TPU v7x, 256 devices: a whole 4x4x8 slice. The times are simulated.
256 devices in a mesh: ctx: 64 (over y_lo, z, x), wt: 4 (over y_hi, core).
Axes of the slice: x: 4, y: 4 (y_hi: 2, y_lo: 2; y = y_hi * 2 + y_lo), z: 8, core: 2. Of those that a mesh axis runs over, the one named last changes fastest.
Arguments:
- tokens: bfloat16 [32768, 4096], P('ctx'), may hold values from -6 to 6
- round_var: float32 [4096, 4096], P('ctx', 'wt'), may hold values from -6 to 6
- grid_base: bfloat16 [4096, 4096], P('ctx', 'wt'), may hold values from -8 to 7, as said below
- col_scale: float32 [4096], P('wt'), may hold values from 0.0015 to 0.006
- queries: bfloat16 [32768, 4096], P('ctx', 'wt'), may hold values from -4 to 4
- keys: bfloat16 [32768, 4096], P('ctx', 'wt'), may hold values from -4 to 4
- gates: bfloat16 [32768, 4096], P('ctx', 'wt'), may hold values from -6 to 6
- target: bfloat16 [32768, 4096], P('ctx', 'wt'), may hold values from -6 to 6
- decay_code: int32 [32], P('wt'), may hold values from 7 to 19
- boundary: int32 [128], P('ctx'), may hold values from 0 to 1, as said below
Outputs:
- gated_out: bfloat16 [32768, 4096], P('ctx', 'wt')
- rounding_grad: float32 [4096, 4096], P('ctx', 'wt')
Inputs may be any that keep to these rules, and one draw needn't show every extreme that they name: `grid_base`: integer grid levels. At least one group begins after a segment boundary.
All inputs are finite; a program needn't handle non-finite values.
Results may differ from a plain program's by a relative error of at most 0.011.
Values may be sent and summed in bfloat16 or wider, within the bound.
A program may use at most 128 MiB of HBM per device.

v0:
```python
import math

import jax
import jax.numpy as jnp
from jax import lax
from jax.sharding import PartitionSpec as P

HEADS = 32
HEAD = 128
GROUP = 256


epsilon = 1e-06
loss_weight = 1024.0


def carried_in(part, axis, combine, identity, reverse):
    count = lax.axis_size(axis)
    place = lax.axis_index(axis)
    ahead = count - 1 - place if reverse else place
    gathered = jax.tree.map(lambda a: lax.all_gather(a, axis), part)
    state = jax.tree.map(lambda a, e: jnp.zeros_like(a) + jnp.asarray(e, a.dtype), part, identity)

    def one(step, state):
        source = count - 1 - step if reverse else step
        return combine(
            state, jax.tree.map(lambda a: lax.dynamic_index_in_dim(a, source, 0, False), gathered)
        )

    return lax.fori_loop(0, ahead, one, state)


def combine(earlier, later):
    return (earlier[0] * later[0], later[0][:, None, None] * earlier[1] + later[1])


def tables(decay_code):
    decay_rate = jnp.exp2(-decay_code.astype(jnp.float32))
    offsets = jnp.arange(GROUP).astype(jnp.float32)
    query_decay = jnp.exp(-offsets[:, None] * decay_rate[None, :])
    key_decay = jnp.exp(-(GROUP - offsets)[:, None] * decay_rate[None, :])
    spacing = offsets[:, None] - offsets[None, :]
    causal_decay = jnp.where(
        spacing[None] >= 0.0,
        jnp.exp(-jnp.maximum(spacing, 0.0)[None] * decay_rate[:, None, None]),
        0.0,
    )
    group_decay = jnp.exp(-GROUP * decay_rate)
    return (query_decay, key_decay, causal_decay, group_decay)


def on_device(
    tokens, round_var, grid_base, col_scale, queries, keys, gates, target, decay_code, boundary
):
    squash = jax.nn.sigmoid(round_var)
    raw_level = 1.2 * squash - 0.1
    soft_part = jnp.clip(raw_level, 0.0, 1.0)
    slopes = jnp.where((raw_level > 0.0) & (raw_level < 1.0), 1.2 * squash * (1.0 - squash), 0.0)
    weight = (col_scale[None, :] * (grid_base.astype(jnp.float32) + soft_part)).astype(jnp.bfloat16)
    rows_here = tokens.shape[0]
    col_count = queries.shape[1]
    head_count = col_count // HEAD
    blocks = rows_here // GROUP
    ctx_count = lax.axis_size("ctx")
    projected = jnp.dot(
        tokens,
        lax.all_gather(weight, "ctx", axis=0, tiled=True),
        preferred_element_type=jnp.float32,
    )
    shape4 = (blocks, GROUP, head_count, HEAD)
    value_all = projected.astype(jnp.bfloat16).reshape(shape4)
    query_all = queries.reshape(shape4)
    key_all = keys.reshape(shape4)
    query_decay, key_decay, causal_decay, group_decay = tables(decay_code)
    scores = jnp.einsum("cihd,cjhd->chij", query_all, key_all, preferred_element_type=jnp.float32)
    weights = (scores * causal_decay[None]).astype(jnp.bfloat16)
    query_dec = (query_all * query_decay[None, :, :, None]).astype(jnp.bfloat16)
    key_dec = (key_all * key_decay[None, :, :, None]).astype(jnp.bfloat16)
    intra = jnp.einsum("chij,cjhe->cihe", weights, value_all, preferred_element_type=jnp.float32)
    updates = jnp.einsum("cjhd,cjhe->chde", key_dec, value_all, preferred_element_type=jnp.float32)
    multiplier = 1.0 - 0.5 * boundary.astype(jnp.float32)
    local_state = jnp.zeros((head_count, HEAD, HEAD), jnp.float32)
    state_coef = jnp.ones((head_count,), jnp.float32)
    local_list = []
    coef_list = []
    for block in range(blocks):
        state_coef = state_coef * multiplier[block]
        local_state = multiplier[block] * local_state
        local_list.append(local_state)
        coef_list.append(state_coef)
        local_state = group_decay[:, None, None] * local_state + updates[block]
        state_coef = state_coef * group_decay
    prefix = carried_in(
        (state_coef, local_state),
        "ctx",
        combine,
        (jnp.ones_like(state_coef), jnp.zeros_like(local_state)),
        False,
    )
    entering = prefix[1]
    states = jnp.stack(
        [
            part_state + part_coef[:, None, None] * entering
            for part_state, part_coef in zip(local_list, coef_list)
        ]
    )
    attn_all = intra + jnp.einsum(
        "cihd,chde->cihe",
        query_dec,
        states.astype(jnp.bfloat16),
        preferred_element_type=jnp.float32,
    )
    attn = attn_all.reshape(rows_here, col_count)
    row_squares = lax.psum(jnp.sum(attn * attn, axis=1), "wt")
    rms = jnp.sqrt(row_squares / (HEADS * HEAD) + epsilon)
    normed = attn / rms[:, None]
    gate_open = jax.nn.sigmoid(gates.astype(jnp.float32))
    gated = normed * gate_open
    gated_out = gated.astype(jnp.bfloat16)
    grad_gated = (gated - target.astype(jnp.float32)) * (
        loss_weight / math.sqrt(rows_here * ctx_count)
    )
    grad_normed = grad_gated * gate_open
    row_inner = lax.psum(jnp.sum(grad_normed * normed, axis=1), "wt")
    grad_attn = (
        (grad_normed - normed * (row_inner / (HEADS * HEAD))[:, None]) / rms[:, None]
    ).astype(jnp.bfloat16)
    grad_all = grad_attn.reshape(shape4)
    back_intra = jnp.einsum(
        "chij,cihe->cjhe", weights, grad_all, preferred_element_type=jnp.float32
    )
    collected = jnp.einsum(
        "cihd,cihe->chde", query_dec, grad_all, preferred_element_type=jnp.float32
    )
    later_local = jnp.zeros((head_count, HEAD, HEAD), jnp.float32)
    later_coef = jnp.ones((head_count,), jnp.float32)
    next_list = [None] * blocks
    next_coefs = [None] * blocks
    for block in reversed(range(blocks)):
        next_list[block] = later_local
        next_coefs[block] = later_coef
        later_local = multiplier[block] * (
            collected[block] + group_decay[:, None, None] * later_local
        )
        later_coef = later_coef * group_decay * multiplier[block]
    suffix = carried_in(
        (later_coef, later_local),
        "ctx",
        combine,
        (jnp.ones_like(later_coef), jnp.zeros_like(later_local)),
        True,
    )
    from_later = suffix[1]
    next_states = jnp.stack(
        [
            part_state + part_coef[:, None, None] * from_later
            for part_state, part_coef in zip(next_list, next_coefs)
        ]
    )
    grad_values = back_intra + jnp.einsum(
        "cjhd,chde->cjhe",
        key_dec,
        next_states.astype(jnp.bfloat16),
        preferred_element_type=jnp.float32,
    )
    grad_values = grad_values.astype(jnp.bfloat16).reshape(rows_here, col_count)
    full_term = lax.dot_general(
        tokens, grad_values, (((0,), (0,)), ((), ())), preferred_element_type=jnp.float32
    )
    weight_grad = lax.psum_scatter(full_term, "ctx", scatter_dimension=0, tiled=True)
    rounding_grad = col_scale[None, :] * slopes * weight_grad
    return (gated_out, rounding_grad)


def solution(mesh):
    placed = (
        P("ctx", None),
        P("ctx", "wt"),
        P("ctx", "wt"),
        P("wt"),
        P("ctx", "wt"),
        P("ctx", "wt"),
        P("ctx", "wt"),
        P("ctx", "wt"),
        P("wt"),
        P("ctx"),
    )
    return jax.shard_map(
        on_device,
        mesh=mesh,
        in_specs=placed,
        out_specs=(P("ctx", "wt"), P("ctx", "wt")),
        check_vma=False,
    )
```

profile of v0, /device:TPU:8, one launch (start us, length us, event | category | flops | bytes accessed | tf_op | source)
XLA Modules:
  0.0 1664.9 jit_solution(1325036017043877112)
XLA Ops:
  7.2 1.8 multiply_convert_fusion.7
  9.1 1.5 copy.66
  13.8 1.3 broadcast_multiply_fusion.1
  15.1 307.0 %all-gather.6.cloned.1.call-done = bf16[4096,1024]{1,0:T(8,128)(2,1)} async-done(((bf16[64,1024]{1,0:T(8,128)(2,1)}), bf16[4096,1024]{1,0:T(8,128)(2,1)}) %all-gather.6.cloned.1.call-update) | async-done | bytes 8388624 | tf_op jit(solution)/shard_map/all_gather | solution.py:67
  322.1 9.1 fusion
  332.5 1.3 fusion.11
  333.8 1.5 slice_add_fusion.1
  335.3 1.3 multiply_dynamic-update-slice_fusion
  336.6 160.3 %all-reduce.2 = (f32[512]{0:T(512)S(1)}, f32[512]{0:T(512)S(1)}) all-reduce(f32[512]{0:T(512)S(1)} %get-tuple-element.170, f32[512]{0:T(512)S(1)} %multiply_dynamic-update-slice_fusion), channel_id=2, replica_groups=mesh['ctx'=64,'wt'=4] {'ctx'}, use_global_device_ids=true, to_apply=%add | all-reduce | flops 1024 | bytes 8192
  497.0 1.5 copy.65
  498.5 1.5 copy.50
  502.5 2.1 fusion.34
  504.6 208.0 %all-gather.8.cloned.1.call-done = f32[64,8,128,128]{3,2,1,0:T(8,128)} async-done(((f32[1,8,128,128]{3,2,1,0:T(8,128)}), f32[64,8,128,128]{3,2,1,0:T(8,128)}) %all-gather.8.cloned.1.call-update) | async-done | bytes 33554448 | tf_op jit(solution)/shard_map/all_gather | solution.py:21
  712.6 39.4 %while.26 = (s32[]{:T(128)}, f32[8,128,128]{2,1,0:T(8,128)S(1)}, s32[]{:T(128)}, f32[64,8]{1,0:T(8,128)S(1)}, f32[64,8,128,128]{3,2,1,0:T(8,128)}, /*index=5*/s32[]{:T(128)}, s32[]{:T(128)}, s32[]{:T(128)}) while((s32[]{:T(128)}, f32[8,128,128]{2,1,0:T(8,128)S(1)}, s32[]{:T(128)}, f32[64,8]{1,0:T(8,128)S(1)}, f32[64,8,128,128]{3,2,1,0:T(8,128)}, ...), condition=%wide.region_1.2_spmd, body=%wide.region_0.1_spmd.sunk | while | flops 262149 | bytes 1573095 | solution.py:30
  712.7 1.2 bitcast_add_fusion.6
  713.9 1.2 bitcast_add_fusion.6
  715.1 1.2 bitcast_add_fusion.6
  716.4 1.2 bitcast_add_fusion.6
  717.6 1.2 bitcast_add_fusion.6
  718.8 1.2 bitcast_add_fusion.6
  720.1 1.2 bitcast_add_fusion.6
  721.3 1.2 bitcast_add_fusion.6
  722.5 1.2 bitcast_add_fusion.6
  723.8 1.2 bitcast_add_fusion.6
  725.0 1.2 bitcast_add_fusion.6
  726.2 1.2 bitcast_add_fusion.6
  727.5 1.2 bitcast_add_fusion.6
  728.7 1.2 bitcast_add_fusion.6
  729.9 1.2 bitcast_add_fusion.6
  731.2 1.2 bitcast_add_fusion.6
  732.4 1.2 bitcast_add_fusion.6
  733.6 1.2 bitcast_add_fusion.6
  734.8 1.2 bitcast_add_fusion.6
  736.1 1.2 bitcast_add_fusion.6
  737.3 1.2 bitcast_add_fusion.6
  738.5 1.2 bitcast_add_fusion.6
  739.8 1.2 bitcast_add_fusion.6
  741.0 1.2 bitcast_add_fusion.6
  742.2 1.2 bitcast_add_fusion.6
  748.4 1.2 bitcast_add_fusion.6
  752.1 2.5 fusion.27
  754.5 3.5 multiply_reduce_fusion.1
  758.0 7.1 psum.14
  765.2 3.0 copy.53
  768.2 3.0 multiply_reduce_fusion
  771.2 9.5 psum.15
  780.7 4.1 fusion.4
  787.5 2.1 fusion.12
  789.8 1.8 fusion.6
  791.6 405.3 %all-gather.10.cloned.1.call-done = f32[64,8,128,128]{3,2,1,0:T(8,128)} async-done(((f32[1,8,128,128]{3,2,1,0:T(8,128)}), f32[64,8,128,128]{3,2,1,0:T(8,128)}) %all-gather.10.cloned.1.call-update) | async-done | bytes 33554448 | tf_op jit(solution)/shard_map/all_gather | solution.py:21
  1196.9 38.3 %while.27 = (s32[]{:T(128)}, f32[8,128,128]{2,1,0:T(8,128)S(1)}, s32[]{:T(128)}, f32[64,8]{1,0:T(8,128)S(1)}, f32[64,8,128,128]{3,2,1,0:T(8,128)}, /*index=5*/s32[]{:T(128)}, s32[]{:T(128)}, s32[]{:T(128)}, s32[]{:T(128)}) while((s32[]{:T(128)}, f32[8,128,128]{2,1,0:T(8,128)S(1)}, s32[]{:T(128)}, f32[64,8]{1,0:T(8,128)S(1)}, ...), condition=%wide.region_7.8_spmd, body=%wide.region_6.7_spmd.sunk | while | flops 262150 | bytes 1573115 | solution.py:30
  1197.0 1.3 bitcast_add_fusion.7
  1198.3 1.2 bitcast_add_fusion.7
  1215.6 1.2 bitcast_add_fusion.7
  1216.8 1.2 bitcast_add_fusion.7
  1218.0 1.2 bitcast_add_fusion.7
  1219.3 1.2 bitcast_add_fusion.7
  1220.5 1.2 bitcast_add_fusion.7
  1221.7 1.2 bitcast_add_fusion.7
  1235.3 1.9 fusion.29
  1238.7 10.4 convolution_bitcast_fusion
  1249.1 17.4 %copy.63 = f32[4096,1024]{1,0:T(8,128)} copy(f32[4096,1024]{0,1:T(8,128)} %convolution_bitcast_fusion) | data formatting | bytes 33554432
  1266.6 390.0 %reduce-scatter.4.cloned.1.call-done = f32[64,1024]{1,0:T(8,128)} async-done(((f32[4096,1024]{1,0:T(8,128)}), f32[64,1024]{1,0:T(8,128)}) %reduce-scatter.4.cloned.1.call-update) | async-done | bytes 262160 | tf_op jit(solution)/shard_map/reduce_scatter | solution.py:170
  1656.6 1.8 multiply_multiply_fusion.1
  (158 shorter events, 45.4 us)
Async XLA Ops:
  7.2 3.5 copy-start.15
  7.2 4.8 copy-start.14
  7.2 6.0 copy-start.13
  7.2 314.9 %all-gather.6.cloned.1.call-start = ((), (), s32[]{:S(2)}) async-start(), calls=%async_computation.1 | async-start | bytes 8519680 | tf_op jit(solution)/shard_map/all_gather | solution.py:67
  9.1 703.5 %all-gather.8.cloned.1.call-start = ((), (), s32[]{:S(2)}) async-start(), calls=%async_computation.2 | async-start | bytes 34078720 | tf_op jit(solution)/shard_map/all_gather | solution.py:21
  10.6 490.0 %copy-start = (bf16[64,8,8,128]{3,2,1,0:T(8,128)(2,1)}, bf16[64,8,8,128]{3,2,1,0:T(8,128)(2,1)S(1)}, u32[]{:S(2)}) copy-start(bf16[64,8,8,128]{3,2,1,0:T(8,128)(2,1)S(1)} %copy.66) | copy-start | bytes 3145732
  332.4 2.8 copy-start.5
  333.7 164.8 %copy-start.8 = (f32[2,8,128,128]{3,2,1,0:T(8,128)}, f32[2,8,128,128]{3,2,1,0:T(8,128)S(1)}, u32[]{:S(2)}) copy-start(f32[2,8,128,128]{3,2,1,0:T(8,128)S(1)} %fusion.11) | copy-start | bytes 3145732
  335.3 861.6 %all-gather.10.cloned.1.call-start = ((), (), s32[]{:S(2)}) async-start(), calls=%async_computation.3 | async-start | bytes 34078720 | tf_op jit(solution)/shard_map/all_gather | solution.py:21
  500.0 1.2 copy-start.2
  501.2 1.2 copy-start.6
  752.1 2.5 copy-start.3
  765.2 3.0 copy-start.10
  784.8 1.2 copy-start.4
  786.5 1.0 copy-start.9
  789.6 867.0 %reduce-scatter.4.cloned.1.call-start = ((), (), s32[]{:S(2)}) async-start(), calls=%async_computation.4 | async-start | bytes 17039360 | tf_op jit(solution)/shard_map/reduce_scatter | solution.py:170
  1196.9 40.2 %copy-start.7 = (f32[2,8,128,256]{3,2,1,0:T(8,128)S(1)}, f32[2,8,128,256]{3,2,1,0:T(8,128)}, u32[]{:S(2)}) copy-start(f32[2,8,128,256]{3,2,1,0:T(8,128)} %fusion.6) | copy-start | bytes 6291460
  1235.3 1.9 copy-start.1
  1266.5 390.1 %copy-start.11 = (f32[64,1024]{1,0:T(8,128)S(1)}, f32[64,1024]{1,0:T(8,128)}, u32[]{:S(2)}) copy-start(f32[64,1024]{1,0:T(8,128)} %param.15) | copy-start | bytes 786436
  1266.5 390.1 %copy-start.12 = (f32[1024]{0:T(1024)S(1)}, f32[1024]{0:T(1024)}, u32[]{:S(2)}) copy-start(f32[1024]{0:T(1024)} %param.17) | copy-start | bytes 12292
Sparse Core Ops, SparseCore 0:
  10.4 311.7 all-gather.5
  335.4 377.1 all-gather.7
  789.7 407.0 all-gather.9
  1266.7 389.8 reduce-scatter.3
where the time goes:
time: 1670 us; the launch traced here: 1660 us
  waiting for transfers between devices  1310 us (78%)
  blocking collectives  177 us (11%)
  other arithmetic  97.5 us (6%)
  local copies, waits for them, and re-layouts  32.3 us (2%)
  matrix products  30.2 us (2%)
    all_gather x2, waiting for transfers between devices, carried_in(): gathered = jax.tree.map(lambda a: lax.all_gather(a, axis), part)  613 us
    reduce_scatter x1, waiting for transfers between devices, on_device(): lax.psum_scatter(full_term, 'ctx', scatter_dimension=0, tiled=True)  390 us
    all_gather x1, waiting for transfers between devices, on_device(): lax.all_gather(weight, 'ctx', axis=0, tiled=True)  307 us
    unnamed x1, blocking collectives  160 us
    add x63, other arithmetic, combine(): later[0][:, None, None] * earlier[1] + later[1]  75.1 us
  transfers between devices with their start and end apart: 4, of which 4 were waited for; matrix products, arithmetic and copies ran while one was open for 1% of the time, Pallas kernels for 0%

commit v1 on v0

--- a/solution.py
+++ b/solution.py
@@ -1,9 +1,525 @@
-import math
-
+import functools, heapq, math
 import jax
 import jax.numpy as jnp
 from jax import lax
 from jax.sharding import PartitionSpec as P
+from jax.experimental import pallas as pl
+from jax.experimental.pallas import tpu as pltpu
+
+MESH = pl.DeviceIdType.MESH
+NX, NZ, NY = 4, 8, 2
+SPLIT = 384
+BF = jnp.bfloat16
+F32 = jnp.float32
+
+
+def place():
+    ctx = lax.axis_index("ctx")
+    wt = lax.axis_index("wt")
+    x = lax.rem(ctx, NX)
+    z = lax.rem(lax.div(ctx, NX), NZ)
+    y = lax.div(ctx, NX * NZ)
+    return x, y, z, wt
+
+
+def at(x, y, z, wt):
+    return (y * (NX * NZ) + z * NX + x, wt)
+
+
+def meet(peers):
+    barrier = pltpu.get_barrier_semaphore()
+    for peer in peers:
+        pl.semaphore_signal(barrier, inc=1, device_id=peer, device_id_type=MESH)
+    pl.semaphore_wait(barrier, len(peers))
+
+
+def scan_kernel(reverse, part_ref, rate_ref, out_ref, xbuf, pref, tbuf, ybuf, zbuf, rbuf, obuf,
+                s1, r1, s2, r2, s3, r3, s4, r4):
+    x, y, z, wt = place()
+    j = y * NZ + z
+    rows = [lax.rem(x + k, NX) for k in range(1, NX)]
+    cols = [lax.rem(j + k, NY * NZ) for k in range(1, NY * NZ)]
+    row_dev = [at(p, y, z, wt) for p in rows]
+    col_dev = [at(x, lax.div(p, NZ), lax.rem(p, NZ), wt) for p in cols]
+    meet(row_dev + col_dev)
+
+    def go(src, dst, ssem, rsem, dev):
+        c = pltpu.make_async_remote_copy(
+            src_ref=src, dst_ref=dst, send_sem=ssem, recv_sem=rsem, device_id=dev, device_id_type=MESH
+        )
+        c.start()
+        return c
+
+    one = [
+        go(part_ref.at[p], xbuf.at[x], s1.at[k], r1.at[k], d)
+        for k, (p, d) in enumerate(zip(rows, row_dev))
+    ]
+    xbuf[x] = part_ref[x]
+    rate = rate_ref[pl.ds(x * 16, 16)]
+    rate1 = rate_ref[x * 16 + j]
+    rate4 = (rate1 * rate1) * (rate1 * rate1)
+    for c in one:
+        c.wait_recv()
+    order = list(reversed(range(NX))) if reverse else list(range(NX))
+    total = jnp.zeros((16, 16, 128), F32)
+    mult = jnp.ones((16, 128), F32)
+    mults = []
+    for i in order:
+        pref[i] = total
+        mults.append(mult)
+        m = xbuf[i, 16].astype(F32)
+        total = (rate * m[None]) * total + xbuf[i, pl.ds(0, 16)].astype(F32)
+        mult = mult * m
+    tbuf[:, 0] = total.astype(BF)
+    tbuf[:, 1] = jnp.broadcast_to(mult.astype(BF)[None], (16, 16, 128))
+    two = [
+        go(tbuf.at[p], ybuf.at[j], s2.at[k], r2.at[k], d)
+        for k, (p, d) in enumerate(zip(cols, col_dev))
+    ]
+    ybuf[j] = tbuf[j]
+    for c in two:
+        c.wait_recv()
+    state = jnp.zeros((16, 128), F32)
+    span = NY * NZ
+    for i in (reversed(range(span)) if reverse else range(span)):
+        zbuf[i] = state.astype(BF)
+        state = (rate4 * ybuf[i, 1].astype(F32)) * state + ybuf[i, 0].astype(F32)
+    three = [
+        go(zbuf.at[p], rbuf.at[j], s3.at[k], r3.at[k], d)
+        for k, (p, d) in enumerate(zip(cols, col_dev))
+    ]
+    rbuf[j] = zbuf[j]
+    for c in three:
+        c.wait_recv()
+    entering = rbuf[...].astype(F32)
+    grow = jnp.ones((16, 1, 128), F32)
+    for n, i in enumerate(order):
+        obuf[i] = (pref[i] + (grow * mults[n][None]) * entering).astype(BF)
+        grow = grow * rate
+    four = [
+        go(obuf.at[p], out_ref.at[x], s4.at[k], r4.at[k], d)
+        for k, (p, d) in enumerate(zip(rows, row_dev))
+    ]
+    out_ref[x] = obuf[x]
+    for c in four:
+        c.wait_recv()
+    for c in one + two + three + four:
+        c.wait_send()
+
+
+def scan_states(part, mult, rate2, reverse):
+    quarters = part.astype(BF).reshape(NX, 16, 16, 128)
+    tile = jnp.broadcast_to(mult.astype(BF), (NX, 1, 16, 128))
+    packed = jnp.concatenate([quarters, tile], axis=1)
+    rates = jnp.broadcast_to(rate2[:, None, None, None], (8, 8, 1, 128)).reshape(64, 1, 128)
+    vm = pl.BlockSpec(memory_space=pltpu.VMEM)
+    out = pl.pallas_call(
+        functools.partial(scan_kernel, reverse),
+        out_shape=jax.ShapeDtypeStruct((NX, 16, 16, 128), BF),
+        in_specs=[vm, vm],
+        out_specs=vm,
+        scratch_shapes=[
+            pltpu.VMEM((NX, 17, 16, 128), BF),
+            pltpu.VMEM((NX, 16, 16, 128), F32),
+            pltpu.VMEM((16, 2, 16, 128), BF),
+            pltpu.VMEM((16, 2, 16, 128), BF),
+            pltpu.VMEM((16, 16, 128), BF),
+            pltpu.VMEM((16, 16, 128), BF),
+            pltpu.VMEM((NX, 16, 16, 128), BF),
+        ]
+        + [pltpu.SemaphoreType.DMA((n,)) for n in (3, 3, 15, 15, 15, 15, 3, 3)],
+        compiler_params=pltpu.CompilerParams(collective_id=2 if reverse else 1, has_side_effects=True),
+        name="state_scan_back" if reverse else "state_scan",
+    )(packed, rates)
+    return out.reshape(8, 128, 128)
+
+
+LAT = 1.7
+RATE = 90e3 / 2
+
+
+class Links:
+    def __init__(self):
+        self.free = {}
+
+    def send(self, link, now, nbytes):
+        start = max(now, self.free.get(link, 0.0))
+        done = start + nbytes / RATE
+        self.free[link] = done
+        return done + LAT
+
+
+def gather_plan():
+    width = {0: SPLIT, 1: 1024 - SPLIT}
+    links = Links()
+    heap = []
+    plan = []
+    seq = [0]
+    have = {}
+
+    def push(link, now, key, halves):
+        color, oz, ox, _ = key
+        nbytes = halves * 64 * width[color] * 2
+        seq[0] += 1
+        heapq.heappush(heap, (links.send(link, now, nbytes), seq[0], link, key))
+        return seq[0] - 1
+
+    def sends_for(color, link, oz, ox):
+        out = []
+        axis = link[0]
+        first, second = ("x", "z") if color == 0 else ("z", "x")
+        size = {"x": NX, "z": NZ}
+        off = {"x": ox, "z": oz}
+        if axis in "xz":
+            dist = abs(off[axis])
+            if dist < size[axis] // 2:
+                out.append((link, 0 if link[1] == "+" else 1) if dist == size[axis] // 2 - 1 else (link, None))
+        if axis == "y":
+            out += [(first + "+", None), (first + "-", None)]
+        if axis in ("y", first):
+            out += [(second + "+", None), (second + "-", None)]
+        return out
+
+    def emit(now, color, link, oz, ox, skip_second=False):
+        for nxt, half in sends_for(color, link, oz, ox):
+            if skip_second and nxt[0] != link[0]:
+                continue
+            step = 1 if nxt[1] == "+" else -1
+            n_oz = oz - step if nxt[0] == "z" else oz
+            n_ox = ox - step if nxt[0] == "x" else ox
+            sid = push(nxt, now, (color, n_oz, n_ox, half), 1 if half is not None else 2)
+            plan.append(("send", sid, color, nxt, oz, ox, half))
+
+    for color in (1, 0):
+        sid = push("y", 0.0, (color, 0, 0, None), 1)
+        plan.append(("send", sid, color, "y", 0, 0, None))
+    count = {}
+    parts = {}
+    while heap:
+        now, sq, link, key = heapq.heappop(heap)
+        color, oz, ox, half = key
+        first = "x" if color == 0 else "z"
+        plan.append(("recv", sq - 1))
+        size = {"x": NX, "z": NZ, "y": 2}[link[0]]
+        whole = True
+        if half is not None:
+            spot = (color, oz % NZ, ox % NX)
+            parts[spot] = parts.get(spot, 0) + 1
+            whole = parts[spot] == 2
+            if whole and link[0] == first:
+                second = "z" if color == 0 else "x"
+                for sign in "+-":
+                    step = 1 if sign == "+" else -1
+                    n_oz = oz - step if second == "z" else oz
+                    n_ox = ox - step if second == "x" else ox
+                    sid = push(second + sign, now, (color, n_oz, n_ox, None), 2)
+                    plan.append(("send", sid, color, second + sign, oz, ox, None))
+        else:
+            emit(now, color, link, oz, ox)
+        if whole:
+            spot = (color, oz % NZ)
+            count[spot] = count.get(spot, 0) + 1
+            if count[spot] == NX:
+                plan.append(("product", color, oz % NZ))
+    return plan, seq[0], max(links.free.values())
+
+
+def gather_kernel(plan, tok_ref, w_ref, out_ref, wa, wb, acc, ssem, rsem):
+    x, y, z, wt = place()
+    peers = {
+        "x+": at(lax.rem(x + 1, NX), y, z, wt),
+        "x-": at(lax.rem(x + NX - 1, NX), y, z, wt),
+        "z+": at(x, y, lax.rem(z + 1, NZ), wt),
+        "z-": at(x, y, lax.rem(z + NZ - 1, NZ), wt),
+        "y": at(x, 1 - y, z, wt),
+    }
+    meet(list(peers.values()))
+    buf = (wa, wb)
+    lanes = ((0, SPLIT), (SPLIT, 1024))
+    copies = {}
+    for op in plan:
+        if op[0] == "send":
+            _, sid, color, link, oz, ox, half = op
+            w = buf[color]
+            if link == "y":
+                lo, hi = lanes[color]
+                src = w_ref.at[:, lo:hi]
+                dst = w.at[y, z, x]
+            else:
+                zz = lax.rem(z + (oz + 2 * NZ), NZ)
+                xx = lax.rem(x + (ox + 2 * NX), NX)
+                dst = w.at[:, zz, xx] if half is None else w.at[half, zz, xx]
+                src = dst
+            c = pltpu.make_async_remote_copy(
+                src_ref=src, dst_ref=dst, send_sem=ssem.at[sid], recv_sem=rsem.at[sid],
+                device_id=peers[link], device_id_type=MESH,
+            )
+            c.start()
+            copies[sid] = c
+            if len(copies) == 2:
+                wa[y, z, x] = w_ref[:, :SPLIT]
+                wb[y, z, x] = w_ref[:, SPLIT:]
+                acc[...] = jnp.zeros_like(acc)
+        elif op[0] == "recv":
+            copies[op[1]].wait_recv()
+        else:
+            _, color, oz = op
+            zz = lax.rem(z + oz, NZ)
+            lo, hi = lanes[color]
+            w = buf[color]
+
+            @pl.loop(0, 4)
+            def _(i, zz=zz, lo=lo, hi=hi, w=w):
+                r = pl.ds(pl.multiple_of(i * 128, 128), 128)
+                t0 = tok_ref[r, pl.ds(pl.multiple_of(zz * 256, 256), 256)]
+                t1 = tok_ref[r, pl.ds(pl.multiple_of(zz * 256 + 2048, 256), 256)]
+                acc[r, lo:hi] += jnp.dot(
+                    t0, w[0, zz].reshape(256, hi - lo), preferred_element_type=F32
+                ) + jnp.dot(t1, w[1, zz].reshape(256, hi - lo), preferred_element_type=F32)
+    out_ref[...] = acc[...].astype(BF)
+    for c in copies.values():
+        c.wait_send()
+
+
+def project(tokens, weight):
+    plan, n, _ = gather_plan()
+    vm = pl.BlockSpec(memory_space=pltpu.VMEM)
+    return pl.pallas_call(
+        functools.partial(gather_kernel, plan),
+        out_shape=jax.ShapeDtypeStruct((512, 1024), BF),
+        in_specs=[vm, vm],
+        out_specs=vm,
+        scratch_shapes=[
+            pltpu.VMEM((NY, NZ, NX, 64, SPLIT), BF),
+            pltpu.VMEM((NY, NZ, NX, 64, 1024 - SPLIT), BF),
+            pltpu.VMEM((512, 1024), F32),
+            pltpu.SemaphoreType.DMA((n,)),
+            pltpu.SemaphoreType.DMA((n,)),
+        ],
+        compiler_params=pltpu.CompilerParams(
+            collective_id=3, has_side_effects=True, vmem_limit_bytes=60 * 2**20
+        ),
+        name="weight_gather_product",
+    )(tokens, weight)
+
+
+CHUNKS = (4, 3, 5, 2, 6, 1, 7, 0)
+CHUNK_US = 1.3
+
+
+def ring(color, stage):
+    axis = ("z", "x") if color == 0 else ("x", "z")
+    return axis[stage - 1], {"x": NX, "z": NZ}[axis[stage - 1]]
+
+
+def reduce_plan():
+    width = {0: SPLIT, 1: 1024 - SPLIT}
+    links = Links()
+    needs = {}
+    inst_of = {(0, 1): (2, 1, 3, 0), (1, 1): CHUNKS, (0, 2): (0,), (1, 2): (0,)}
+    for color in (1, 0):
+        for stage in (1, 2):
+            axis, n = ring(color, stage)
+            for inst in inst_of[color, stage]:
+                for flow in (-1, 1):
+                    for k in range(n // 2, 0, -1):
+                        task = ("s", color, stage, flow, inst, k)
+                        there = (flow * k) % n
+                        if stage == 1:
+                            dep = [("chunk", there if color == 0 else inst)]
+                        else:
+                            dep = [("q", color, 1, there)]
+                        if k < n // 2:
+                            dep.append(("got", color, stage, flow, inst, k + 1))
+                        needs[task] = dep
+                dep = [("got", color, stage, flow, inst, 1) for flow in (-1, 1)]
+                if stage == 1:
+                    dep.append(("chunk", 0 if color == 0 else inst))
+                else:
+                    dep.append(("q", color, 1, 0))
+                needs[("q", color, stage, inst)] = dep
+        needs[("y", color)] = [("q", color, 2, 0)]
+        needs[("out", color)] = [("goty", color)]
+    done = set()
+    plan = []
+    heap = []
+    seq = [0]
+
+    def post(t, event):
+        seq[0] += 1
+        heapq.heappush(heap, (t, seq[0], event))
+
+    for i, oz in enumerate(CHUNKS):
+        post(CHUNK_US * (i + 1), ("chunk", oz))
+    sids = {}
+    last = 0.0
+    while heap:
+        t, _, event = heapq.heappop(heap)
+        last = t
+        done.add(event)
+        if event[0] == "chunk":
+            plan.append(event)
+        moved = True
+        while moved:
+            moved = False
+            for task in list(needs):
+                if all(d in done for d in needs[task]):
+                    del needs[task]
+                    plan.append(task)
+                    moved = True
+                    if task[0] == "s":
+                        _, color, stage, flow, inst, k = task
+                        axis, n = ring(color, stage)
+                        halves = 1 if k == n // 2 else 2
+                        arrive = links.send((axis, flow), t, halves * 64 * width[color] * 2)
+                        post(arrive, ("got",) + task[1:])
+                        sids[task] = len(sids)
+                    elif task[0] == "y":
+                        post(links.send("y", t, 64 * width[task[1]] * 2), ("goty", task[1]))
+                        sids[task] = len(sids)
+                    elif task[0] == "q":
+                        done.add(task)
+    return plan, sids, last
+
+
+def reduce_kernel(plan, sids, tok_ref, gv_ref, factor_ref, out_ref, pa, pb, ra1, rb1, ra2, rb2,
+                  qa, qb, fa, fb, ya, yb, va, vb, ssem, rsem):
+    x, y, z, wt = place()
+    peers = {
+        ("x", 1): at(lax.rem(x + 1, NX), y, z, wt),
+        ("x", -1): at(lax.rem(x + NX - 1, NX), y, z, wt),
+        ("z", 1): at(x, y, lax.rem(z + 1, NZ), wt),
+        ("z", -1): at(x, y, lax.rem(z + NZ - 1, NZ), wt),
+        "y": at(x, 1 - y, z, wt),
+    }
+    meet(list(peers.values()))
+    mine = (pa, pb)
+    quit_ = (qa, qb)
+    slots = {(0, 1): ra1, (1, 1): rb1, (0, 2): ra2, (1, 2): rb2}
+    full = (fa, fb)
+    ysend = (ya, yb)
+    yrecv = (va, vb)
+    lanes = ((0, SPLIT), (SPLIT, 1024))
+    copies = {}
+
+    def slot(color, stage, flow, inst, k):
+        r = slots[color, stage]
+        f = 0 if flow < 0 else 1
+        return r.at[f, inst, k] if stage == 1 else r.at[f, k]
+
+    def own(color, stage, inst, there):
+        if stage == 2:
+            return quit_[color].at[there]
+        oz, ox = (there, inst) if color == 0 else (inst, there)
+        return mine[color].at[:, lax.rem(z + oz, NZ), lax.rem(x + ox, NX)]
+
+    for op in plan:
+        if op[0] == "chunk":
+            zz = lax.rem(z + op[1], NZ)
+
+            @pl.loop(0, 4)
+            def _(i, zz=zz):
+                yy = lax.div(i, 2)
+                h = lax.rem(i, 2)
+                cols = tok_ref[:, pl.ds(pl.multiple_of(yy * 2048 + zz * 256 + h * 128, 128), 128)]
+                r = lax.dot_general(
+                    cols, gv_ref[...], (((0,), (0,)), ((), ())), preferred_element_type=F32
+                ).astype(BF)
+                for u in range(2):
+                    pa[yy, zz, h * 2 + u] = r[u * 64 : u * 64 + 64, :SPLIT]
+                    pb[yy, zz, h * 2 + u] = r[u * 64 : u * 64 + 64, SPLIT:]
+        elif op[0] == "s":
+            _, color, stage, flow, inst, k = op
+            axis, n = ring(color, stage)
+            half = 0 if flow < 0 else 1
+            there = (flow * k) % n
+            p = own(color, stage, inst, there)
+            if k == n // 2:
+                src = p.at[half]
+                dst = slot(color, stage, flow, inst, k - 1).at[half]
+            else:
+                copies["s", color, stage, flow, inst, k + 1].wait_recv()
+                src = slot(color, stage, flow, inst, k)
+                dst = slot(color, stage, flow, inst, k - 1)
+                if k == n // 2 - 1:
+                    src[half] = (src[half].astype(F32) + p[half].astype(F32)).astype(BF)
+                    src[1 - half] = p[1 - half]
+                else:
+                    src[...] = (src[...].astype(F32) + p[...].astype(F32)).astype(BF)
+            sid = sids[op]
+            c = pltpu.make_async_remote_copy(
+                src_ref=src, dst_ref=dst, send_sem=ssem.at[sid], recv_sem=rsem.at[sid],
+                device_id=peers[axis, flow], device_id_type=MESH,
+            )
+            c.start()
+            copies[op] = c
+        elif op[0] == "q":
+            _, color, stage, inst = op
+            for flow in (-1, 1):
+                copies["s", color, stage, flow, inst, 1].wait_recv()
+            low = slot(color, stage, -1, inst, 0)
+            high = slot(color, stage, 1, inst, 0)
+            p = own(color, stage, inst, 0)
+            total = low[...].astype(F32) + high[...].astype(F32) + p[...].astype(F32)
+            if stage == 1:
+                quit_[color][inst] = total.astype(BF)
+            else:
+                full[color][...] = total
+        elif op[0] == "y":
+            color = op[1]
+            ysend[color][...] = full[color][1 - y].astype(BF)
+            sid = sids[op]
+            c = pltpu.make_async_remote_copy(
+                src_ref=ysend[color], dst_ref=yrecv[color], send_sem=ssem.at[sid],
+                recv_sem=rsem.at[sid], device_id=peers["y"], device_id_type=MESH,
+            )
+            c.start()
+            copies[op] = c
+        else:
+            color = op[1]
+            copies["y", color].wait_recv()
+            lo, hi = lanes[color]
+            out_ref[:, lo:hi] = factor_ref[:, lo:hi] * (
+                full[color][y] + yrecv[color][...].astype(F32)
+            )
+    for c in copies.values():
+        c.wait_send()
+
+
+def gradient(tokens, grad_values, factor):
+    plan, sids, _ = reduce_plan()
+    n = len(sids)
+    a, b = SPLIT, 1024 - SPLIT
+    vm = pl.BlockSpec(memory_space=pltpu.VMEM)
+    return pl.pallas_call(
+        functools.partial(reduce_kernel, plan, sids),
+        out_shape=jax.ShapeDtypeStruct((64, 1024), F32),
+        in_specs=[vm, vm, vm],
+        out_specs=vm,
+        scratch_shapes=[
+            pltpu.VMEM((NY, NZ, NX, 64, a), BF),
+            pltpu.VMEM((NY, NZ, NX, 64, b), BF),
+            pltpu.VMEM((2, NX, NZ // 2, NY, 64, a), BF),
+            pltpu.VMEM((2, NZ, NX // 2, NY, 64, b), BF),
+            pltpu.VMEM((2, NX // 2, NY, 64, a), BF),
+            pltpu.VMEM((2, NZ // 2, NY, 64, b), BF),
+            pltpu.VMEM((NX, NY, 64, a), BF),
+            pltpu.VMEM((NZ, NY, 64, b), BF),
+            pltpu.VMEM((NY, 64, a), F32),
+            pltpu.VMEM((NY, 64, b), F32),
+            pltpu.VMEM((64, a), BF),
+            pltpu.VMEM((64, b), BF),
+            pltpu.VMEM((64, a), BF),
+            pltpu.VMEM((64, b), BF),
+            pltpu.SemaphoreType.DMA((n,)),
+            pltpu.SemaphoreType.DMA((n,)),
+        ],
+        compiler_params=pltpu.CompilerParams(
+            collective_id=4, has_side_effects=True, vmem_limit_bytes=60 * 2**20
+        ),
+        name="weight_gradient_reduce",
+    )(tokens, grad_values, factor)
+
 
 HEADS = 32
 HEAD = 128
@@ -12,26 +528,6 @@
 
 epsilon = 1e-06
 loss_weight = 1024.0
-
-
-def carried_in(part, axis, combine, identity, reverse):
-    count = lax.axis_size(axis)
-    place = lax.axis_index(axis)
-    ahead = count - 1 - place if reverse else place
-    gathered = jax.tree.map(lambda a: lax.all_gather(a, axis), part)
-    state = jax.tree.map(lambda a, e: jnp.zeros_like(a) + jnp.asarray(e, a.dtype), part, identity)
-
-    def one(step, state):
-        source = count - 1 - step if reverse else step
-        return combine(
-            state, jax.tree.map(lambda a: lax.dynamic_index_in_dim(a, source, 0, False), gathered)
-        )
-
-    return lax.fori_loop(0, ahead, one, state)
-
-
-def combine(earlier, later):
-    return (earlier[0] * later[0], later[0][:, None, None] * earlier[1] + later[1])
 
 
 def tables(decay_code):
@@ -62,13 +558,8 @@
     head_count = col_count // HEAD
     blocks = rows_here // GROUP
     ctx_count = lax.axis_size("ctx")
-    projected = jnp.dot(
-        tokens,
-        lax.all_gather(weight, "ctx", axis=0, tiled=True),
-        preferred_element_type=jnp.float32,
-    )
     shape4 = (blocks, GROUP, head_count, HEAD)
-    value_all = projected.astype(jnp.bfloat16).reshape(shape4)
+    value_all = project(tokens, weight).reshape(shape4)
     query_all = queries.reshape(shape4)
     key_all = keys.reshape(shape4)
     query_decay, key_decay, causal_decay, group_decay = tables(decay_code)
@@ -90,14 +581,9 @@
         coef_list.append(state_coef)
         local_state = group_decay[:, None, None] * local_state + updates[block]
         state_coef = state_coef * group_decay
-    prefix = carried_in(
-        (state_coef, local_state),
-        "ctx",
-        combine,
-        (jnp.ones_like(state_coef), jnp.zeros_like(local_state)),
-        False,
-    )
-    entering = prefix[1]
+    rate2 = group_decay * group_decay
+    pair = multiplier[0] * multiplier[1]
+    entering = scan_states(local_state, pair, rate2, False).astype(jnp.float32)
     states = jnp.stack(
         [
             part_state + part_coef[:, None, None] * entering
@@ -143,14 +629,7 @@
             collected[block] + group_decay[:, None, None] * later_local
         )
         later_coef = later_coef * group_decay * multiplier[block]
-    suffix = carried_in(
-        (later_coef, later_local),
-        "ctx",
-        combine,
-        (jnp.ones_like(later_coef), jnp.zeros_like(later_local)),
-        True,
-    )
-    from_later = suffix[1]
+    from_later = scan_states(later_local, pair, rate2, True).astype(jnp.float32)
     next_states = jnp.stack(
         [
             part_state + part_coef[:, None, None] * from_later
@@ -164,11 +643,7 @@
         preferred_element_type=jnp.float32,
     )
     grad_values = grad_values.astype(jnp.bfloat16).reshape(rows_here, col_count)
-    full_term = lax.dot_general(
-        tokens, grad_values, (((0,), (0,)), ((), ())), preferred_element_type=jnp.float32
-    )
-    weight_grad = lax.psum_scatter(full_term, "ctx", scatter_dimension=0, tiled=True)
-    rounding_grad = col_scale[None, :] * slopes * weight_grad
+    rounding_grad = gradient(tokens, grad_values, col_scale[None, :] * slopes)
     return (gated_out, rounding_grad)
 
 

time: 1670 us -> 245 us (0.15)
  waiting for transfers between devices: 1310 us -> 0 us
  Pallas kernels: 0 us -> 177 us
  blocking collectives: 177 us -> 16.5 us
  other arithmetic: 97.5 us -> 23.6 us
  matrix products: 30.2 us -> 8.67 us
    all_gather x3 -> x0, waiting for transfers between devices: 920 us -> none  [the longest x2 613 us: carried_in(): gathered = jax.tree.map(lambda a: lax.all_gather(a, axis), part)]
    reduce_scatter x1 -> x0, waiting for transfers between devices: 390 us -> none  [on_device(): lax.psum_scatter(full_term, 'ctx', scatter_dimension=0, tiled=True)]
    pallas_call x0 -> x4, Pallas kernels: none -> 177 us  [the longest x1 65.2 us: project(): pl.pallas_call(functools.partial(gather_kernel, plan), out_shape=jax.Shap...]
    unnamed x1 -> x0, blocking collectives: 160 us -> none
    add x64 -> x0, other arithmetic: 76.6 us -> none  [the longest x63 75.1 us: combine(): later[0][:, None, None] * earlier[1] + later[1]]
    dot_general x2 -> x0, matrix products: 19.5 us -> none  [the longest x1 10.4 us: on_device(): lax.dot_general(tokens, grad_values, (((0,), (0,)), ((), ())), preferred_...]
    unnamed x40 -> x29, local copies, waits for them, and re-layouts: 24.5 us -> 6.33 us
  transfers between devices with their start and end apart: 4 -> 0, of which waited for: 4 -> 0; matrix products, arithmetic and copies ran while one was open for 1% -> 0% of each run, Pallas kernels for 0% -> 0%
where the time goes in v1:
time: 245 us
  Pallas kernels  177 us (72%)
  other arithmetic  23.6 us (10%)
  blocking collectives  16.5 us (7%)
  local copies, waits for them, and re-layouts  15.6 us (6%)
  matrix products  8.67 us (4%)
  between operations  2.86 us (1%)
    pallas_call x1, Pallas kernels, project(): pl.pallas_call(functools.partial(gather_kernel, plan), out_shape=jax.Shap...  65.2 us
    pallas_call x1, Pallas kernels, gradient(): pl.pallas_call(functools.partial(reduce_kernel, plan, sids), out_shape=ja...  57.2 us
    pallas_call x2, Pallas kernels, scan_states(): pl.pallas_call(functools.partial(scan_kernel, reverse), out_shape=jax.Sha...  55.1 us
    psum x1, blocking collectives, on_device(): row_inner = lax.psum(jnp.sum(grad_normed * normed, axis=1), 'wt')  9.36 us
    psum x1, blocking collectives, on_device(): row_squares = lax.psum(jnp.sum(attn * attn, axis=1), 'wt')  7.14 us
    unnamed x29, local copies, waits for them, and re-layouts  6.33 us
    another operation x2, other arithmetic  5.13 us

profile of v1, /device:TPU:8, one launch (start us, length us, event | category | flops | bytes accessed | tf_op | source)
XLA Modules:
  0.0 244.7 jit_solution(15590282021768954962)
XLA Ops:
  0.6 0.7 multiply_subtract_fusion
  1.3 0.6 fusion.29
  1.9 1.3 broadcast_multiply_fusion.2
  3.8 1.3 broadcast_multiply_fusion.1
  5.1 0.1 mul.306
  5.2 0.1 mul.307
  5.3 0.1 mul.308
  5.4 0.1 multiply_exponential_fusion.1
  5.4 1.9 select_multiply_fusion
  7.4 65.2 %weight_gather_product.1 = bf16[512,1024]{1,0:T(8,128)(2,1)} custom-call(bf16[512,4096]{1,0:T(8,128)(2,1)} %tok_ref.3, bf16[64,1024]{1,0:T(8,128)(2,1)} %get-tuple-element.11.w_ref), custom_call_target="tpu_custom_call" | custom-call | tf_op jit(solution)/shard_map/weight_gather_product/pallas_call | solution.py:287
  72.6 0.0 copy-start.8
  72.6 1.6 copy.43
  74.2 0.0 copy-start.5
  74.2 0.0 copy-done.8
  74.2 0.3 copy.45
  74.5 0.0 copy-start.2
  74.5 1.4 fusion.9
  75.9 0.1 fusion.28
  76.0 0.1 mul.299
  76.0 0.1 mul.300
  76.1 0.1 mul.301
  76.2 0.8 add_convert_fusion.2
  78.3 0.7 concatenate.6.part_ref
  79.0 0.1 broadcast_in_dim.22
  79.1 0.1 broadcast_in_dim.23
  79.2 0.8 broadcast_in_dim.24.rate_ref
  79.9 27.4 %state_scan.1 = bf16[4,16,16,128]{3,2,1,0:T(8,128)(2,1)} custom-call(bf16[4,17,16,128]{3,2,1,0:T(8,128)(2,1)} %concatenate.6.part_ref, f32[64,1,128]{2,1,0:T(1,128)} %broadcast_in_dim.24.rate_ref), custom_call_target="tpu_custom_call" | custom-call | tf_op jit(solution)/shard_map/state_scan/pallas_call | solution.py:116
  107.3 0.0 copy-start.9
  107.3 3.2 %fusion.13 = (bf16[1,8,128,128]{3,2,1,0:T(8,128)(2,1)S(1)}, bf16[1,8,128,128]{3,2,1,0:T(8,128)(2,1)}) fusion(bf16[1,8,128,128]{3,2,1,0:T(8,128)(2,1)} %bitcast.65, f32[]{:T(128)} %bitcast, f32[]{:T(128)S(6)} %mul.295, f32[8]{0:T(128)S(1)} %get-tuple-element.16, f32[2,8,128,128]{3,2,1,0:T(8,128)S(1)} %fusion.9, f32[8]{0:T(128)S(1)} %get-tuple-element.17, ...), kind=kLoop, calls=%fused_computation.28 | loop fusion | flops 1179648 | bytes 1310796 | tf_op jit(solution)/shard_map/convert.4
  110.5 0.1 fusion.23
  110.6 0.1 subtract_compare_fusion
  110.8 1.7 exponential_select_fusion
  112.4 0.3 copy.44
  112.7 0.7 copy.31
  113.4 0.0 copy-start.6
  113.4 2.8 %multiply_convert_fusion = bf16[2,8,256,256]{3,2,1,0:T(8,128)(2,1)S(1)} fusion(bf16[2,256,8,128]{1,3,2,0:T(8,128)(2,1)S(1)} %copy.31, f32[8,256,256]{2,1,0:T(8,128)} %exponential_select_fusion, bf16[2,256,8,128]{3,2,1,0:T(8,128)(2,1)} %bitcast.51), kind=kOutput, calls=%fused_computation | convolution fusion | flops 270532608 | bytes 6291456 | tf_op jit(solution)/shard_map/cihd,cjhd->chij/dot_general | solution.py:566
  116.2 0.8 fusion.7
  117.0 0.1 copy-done.10
  117.2 1.9 multiply_reduce_fusion.1
  119.1 2.9 %copy.34 = f32[2,256,8,128]{3,2,1,0:T(8,128)} copy(f32[2,256,8,128]{1,3,2,0:T(8,128)} %get-tuple-element.24) | data formatting | bytes 4194304 | tf_op jit(solution)/shard_map/add | solution.py:593
  122.0 7.1 %psum.14 = f32[512]{0:T(512)S(1)} all-reduce(f32[512]{0:T(512)S(1)} %bitcast.69), channel_id=1, replica_groups=mesh['ctx'=64,'wt'=4] {'wt'}, use_global_device_ids=true, to_apply=%region_1.2 | all-reduce | flops 512 | bytes 4096 | tf_op jit(solution)/shard_map/psum | solution.py:600
  129.2 3.3 %multiply_reduce_fusion = f32[512]{0:T(512)S(1)} fusion(bf16[512,1024]{1,0:T(8,128)(2,1)} %param.17, bf16[512,1024]{1,0:T(8,128)(2,1)} %param.16, f32[512]{0:T(512)S(1)} %add_sqrt_fusion, f32[64,8,8,128]{3,2,1,0:T(8,128)} %bitcast.46), kind=kLoop, calls=%fused_computation.4 | loop fusion | flops 6290944 | bytes 4198400 | tf_op jit(solution)/shard_map/reduce_sum | solution.py:610
  132.5 9.4 %psum.15 = f32[512]{0:T(512)S(1)} all-reduce(f32[512]{0:T(512)S(1)} %multiply_reduce_fusion), channel_id=1, replica_groups=mesh['ctx'=64,'wt'=4] {'wt'}, use_global_device_ids=true, to_apply=%region_3.4 | all-reduce | flops 512 | bytes 4096 | tf_op jit(solution)/shard_map/psum | solution.py:610
  141.9 4.4 %fusion.1 = (bf16[64,8,8,128]{3,1,2,0:T(8,128)(2,1)S(1)}, bf16[512,1024]{1,0:T(8,128)(2,1)}) fusion(f32[512]{0:T(512)S(1)} %add_sqrt_fusion, f32[512]{0:T(512)S(1)} %broadcast_multiply_fusion, bf16[512,1024]{1,0:T(8,128)(2,1)} %param.17, bf16[512,1024]{1,0:T(8,128)(2,1)} %param.16, f32[64,8,8,128]{3,2,1,0:T(8,128)} %bitcast.47), kind=kLoop, calls=%fused_computation.14 | loop fusion | flops 7864320 | bytes 6295552
  146.3 0.3 copy.48
  146.6 0.5 fusion.5
  147.0 1.2 fusion.27
  148.2 0.0 copy-done
  148.2 0.1 copy-done.4
  148.3 0.1 mul.347
  148.4 0.1 mul.348
  148.5 0.1 mul.349
  148.6 2.7 %multiply_convert_fusion.7 = bf16[4,16,16,128]{3,2,1,0:T(8,128)(2,1)S(1)} fusion(f32[4,16,16,128]{3,2,1,0:T(8,128)} %bitcast.64, f32[4,16,16,128]{3,2,1,0:T(8,128)} %bitcast.63, f32[4,16]{1,0:T(4,128)S(1)} %mul.349, f32[]{:T(128)} %bitcast, f32[]{:T(128)} %bitcast.1, f32[4,16]{1,0:T(4,128)S(1)} %mul.301), kind=kLoop, calls=%fused_computation.38 | loop fusion | flops 786432 | bytes 1311240 | tf_op jit(solution)/shard_map/convert_element_type | solution.py:111
  151.3 0.7 concatenate.7.part_ref
  152.1 27.7 %state_scan_back.1 = bf16[4,16,16,128]{3,2,1,0:T(8,128)(2,1)} custom-call(bf16[4,17,16,128]{3,2,1,0:T(8,128)(2,1)} %concatenate.7.part_ref, f32[64,1,128]{2,1,0:T(1,128)} %broadcast_in_dim.24.rate_ref), custom_call_target="tpu_custom_call" | custom-call | tf_op jit(solution)/shard_map/state_scan_back/pallas_call | solution.py:116
  179.8 1.9 add_convert_fusion.1
  181.7 0.5 fusion.3
  182.3 0.7 copy-done.3
  182.9 0.0 copy-done.7
  183.0 0.8 fusion
  183.8 0.8 copy.38
  184.6 1.3 copy.71
  185.8 57.2 %weight_gradient_reduce.1 = f32[64,1024]{1,0:T(8,128)} custom-call(bf16[512,4096]{1,0:T(8,128)(2,1)} %tok_ref.3, bf16[512,1024]{1,0:T(8,128)(2,1)} %bitcast.57, f32[64,1024]{1,0:T(8,128)} %get-tuple-element.10.factor_ref), custom_call_target="tpu_custom_call" | custom-call | tf_op jit(solution)/shard_map/weight_gradient_reduce/pallas_call | solution.py:494
  243.0 1.7 copy.73
  (16 shorter events, 0.0 us)
Async XLA Ops:
  72.6 1.6 copy-start.8
  74.2 1.7 copy-start.5
  74.5 1.5 copy-start.2
  107.3 5.1 %copy-start.9 = (bf16[512,1024]{1,0:T(8,128)(2,1)S(1)}, bf16[512,1024]{1,0:T(8,128)(2,1)}, u32[]{:S(2)}) copy-start(bf16[512,1024]{1,0:T(8,128)(2,1)} %param.14) | copy-start | bytes 3145732
  113.4 2.8 %copy-start.6 = (bf16[64,8,8,128]{3,2,1,0:T(8,128)(2,1)S(1)}, bf16[64,8,8,128]{3,2,1,0:T(8,128)(2,1)}, u32[]{:S(2)}) copy-start(bf16[64,8,8,128]{3,2,1,0:T(8,128)(2,1)} %copy-done.5) | copy-start | bytes 3145732
  116.2 1.0 copy-start.10
  146.6 1.7 copy-start
  147.0 1.3 copy-start.4
  148.3 33.4 %copy-start.1 = (bf16[64,8,8,128]{3,2,1,0:T(8,128)(2,1)S(1)}, bf16[64,8,8,128]{3,2,1,0:T(8,128)(2,1)}, u32[]{:S(2)}) copy-start(bf16[64,8,8,128]{3,2,1,0:T(8,128)(2,1)} %copy-done) | copy-start | bytes 3145732
  181.7 1.2 copy-start.3
  181.7 1.3 copy-start.7

commit v2 on v0

v2 whole, which is shorter than its diff:
```python
import functools, heapq, math
import jax
import jax.numpy as jnp
from jax import lax
from jax.sharding import PartitionSpec as P
from jax.experimental import pallas as pl
from jax.experimental.pallas import tpu as pltpu

MESH = pl.DeviceIdType.MESH
NX, NZ, NY = 4, 8, 2
SPLIT = 384
HEADS = 32
HEAD = 128
GROUP = 256
LANES = ((0, SPLIT), (SPLIT, 1024))
epsilon = 1e-06
loss_weight = 1024.0
BF = jnp.bfloat16
F32 = jnp.float32


def place():
    ctx = lax.axis_index("ctx")
    wt = lax.axis_index("wt")
    x = lax.rem(ctx, NX)
    z = lax.rem(lax.div(ctx, NX), NZ)
    y = lax.div(ctx, NX * NZ)
    return x, y, z, wt


def at(x, y, z, wt):
    return (y * (NX * NZ) + z * NX + x, wt)


LAT = 1.7
RATE = 90e3 / 2


class Links:
    def __init__(self):
        self.free = {}

    def send(self, link, now, nbytes):
        start = max(now, self.free.get(link, 0.0))
        done = start + nbytes / RATE
        self.free[link] = done
        return done + LAT


def gather_plan():
    width = {0: SPLIT, 1: 1024 - SPLIT}
    links = Links()
    heap = []
    plan = []
    seq = [0]
    have = {}

    def push(link, now, key, halves):
        color, oz, ox, _ = key
        nbytes = halves * 64 * width[color] * 2
        seq[0] += 1
        heapq.heappush(heap, (links.send(link, now, nbytes), seq[0], link, key))
        return seq[0] - 1

    def sends_for(color, link, oz, ox):
        out = []
        axis = link[0]
        first, second = ("x", "z") if color == 0 else ("z", "x")
        size = {"x": NX, "z": NZ}
        off = {"x": ox, "z": oz}
        if axis in "xz":
            dist = abs(off[axis])
            if dist < size[axis] // 2:
                out.append((link, 0 if link[1] == "+" else 1) if dist == size[axis] // 2 - 1 else (link, None))
        if axis == "y":
            out += [(first + "+", None), (first + "-", None)]
        if axis in ("y", first):
            out += [(second + "+", None), (second + "-", None)]
        return out

    def emit(now, color, link, oz, ox, skip_second=False):
        for nxt, half in sends_for(color, link, oz, ox):
            if skip_second and nxt[0] != link[0]:
                continue
            step = 1 if nxt[1] == "+" else -1
            n_oz = oz - step if nxt[0] == "z" else oz
            n_ox = ox - step if nxt[0] == "x" else ox
            sid = push(nxt, now, (color, n_oz, n_ox, half), 1 if half is not None else 2)
            plan.append(("send", sid, color, nxt, oz, ox, half))

    for color in (1, 0):
        sid = push("y", 0.0, (color, 0, 0, None), 1)
        plan.append(("send", sid, color, "y", 0, 0, None))
    count = {}
    parts = {}
    while heap:
        now, sq, link, key = heapq.heappop(heap)
        color, oz, ox, half = key
        first = "x" if color == 0 else "z"
        plan.append(("recv", sq - 1))
        size = {"x": NX, "z": NZ, "y": 2}[link[0]]
        whole = True
        if half is not None:
            spot = (color, oz % NZ, ox % NX)
            parts[spot] = parts.get(spot, 0) + 1
            whole = parts[spot] == 2
            if whole and link[0] == first:
                second = "z" if color == 0 else "x"
                for sign in "+-":
                    step = 1 if sign == "+" else -1
                    n_oz = oz - step if second == "z" else oz
                    n_ox = ox - step if second == "x" else ox
                    sid = push(second + sign, now, (color, n_oz, n_ox, None), 2)
                    plan.append(("send", sid, color, second + sign, oz, ox, None))
        else:
            emit(now, color, link, oz, ox)
        if whole:
            spot = (color, oz % NZ)
            count[spot] = count.get(spot, 0) + 1
            if count[spot] == NX:
                plan.append(("product", color, oz % NZ))
    return plan, seq[0], max(links.free.values())


CHUNKS = (4, 3, 5, 2, 6, 1, 7, 0)
CHUNK_US = 1.3


def ring(color, stage):
    axis = ("z", "x") if color == 0 else ("x", "z")
    return axis[stage - 1], {"x": NX, "z": NZ}[axis[stage - 1]]


def reduce_plan():
    width = {0: SPLIT, 1: 1024 - SPLIT}
    links = Links()
    needs = {}
    inst_of = {(0, 1): (2, 1, 3, 0), (1, 1): CHUNKS, (0, 2): (0,), (1, 2): (0,)}
    for color in (1, 0):
        for stage in (1, 2):
            axis, n = ring(color, stage)
            for inst in inst_of[color, stage]:
                for flow in (-1, 1):
                    for k in range(n // 2, 0, -1):
                        task = ("s", color, stage, flow, inst, k)
                        there = (flow * k) % n
                        if stage == 1:
                            dep = [("chunk", there if color == 0 else inst)]
                        else:
                            dep = [("q", color, 1, there)]
                        if k < n // 2:
                            dep.append(("got", color, stage, flow, inst, k + 1))
                        needs[task] = dep
                dep = [("got", color, stage, flow, inst, 1) for flow in (-1, 1)]
                if stage == 1:
                    dep.append(("chunk", 0 if color == 0 else inst))
                else:
                    dep.append(("q", color, 1, 0))
                needs[("q", color, stage, inst)] = dep
        needs[("y", color)] = [("q", color, 2, 0)]
        needs[("out", color)] = [("goty", color)]
    done = set()
    plan = []
    heap = []
    seq = [0]

    def post(t, event):
        seq[0] += 1
        heapq.heappush(heap, (t, seq[0], event))

    for i, oz in enumerate(CHUNKS):
        post(CHUNK_US * (i + 1), ("chunk", oz))
    sids = {}
    last = 0.0
    while heap:
        t, _, event = heapq.heappop(heap)
        last = t
        done.add(event)
        if event[0] == "chunk":
            plan.append(event)
        moved = True
        while moved:
            moved = False
            for task in list(needs):
                if all(d in done for d in needs[task]):
                    del needs[task]
                    plan.append(task)
                    moved = True
                    if task[0] == "s":
                        _, color, stage, flow, inst, k = task
                        axis, n = ring(color, stage)
                        halves = 1 if k == n // 2 else 2
                        arrive = links.send((axis, flow), t, halves * 64 * width[color] * 2)
                        post(arrive, ("got",) + task[1:])
                        sids[task] = len(sids)
                    elif task[0] == "y":
                        post(links.send("y", t, 64 * width[task[1]] * 2), ("goty", task[1]))
                        sids[task] = len(sids)
                    elif task[0] == "q":
                        done.add(task)
    return plan, sids, last


def send(src, dst, ssem, rsem, dev):
    c = pltpu.make_async_remote_copy(
        src_ref=src, dst_ref=dst, send_sem=ssem, recv_sem=rsem, device_id=dev, device_id_type=MESH
    )
    c.start()
    return c


def tdot(a, b):
    return lax.dot_general(a, b, (((0,), (0,)), ((), ())), preferred_element_type=F32)


def layer_kernel(
    gplan, rplan, sids, scale,
    code_ref, bound_ref, rv_ref, gb_ref, cs_ref, tok_hbm, q_hbm, k_hbm, gate_hbm, tgt_hbm,
    gated_hbm, out_ref,
    tok, q, k, gate, tgt, w_own, factor, wa, wb, acc, v, wts, qd, kd, go, ga, gv, hold, rates,
    packed, xbuf, pref, tbuf, ybuf, zbuf, rbuf, obuf, ebuf, sums, got, inv, inn,
    ra1, rb1, ra2, rb2, qa, qb, fa, fb, ya, yb, va, vb,
    lsem, gs, gr, s1, r1, s2, r2, s3, r3, s4, r4, ps, pr, rs, rr,
):
    x, y, z, wt = place()
    j = y * NZ + z
    rows = [lax.rem(x + n, NX) for n in range(1, NX)]
    cols = [lax.rem(j + n, NY * NZ) for n in range(1, NY * NZ)]
    row_dev = [at(p, y, z, wt) for p in rows]
    col_dev = [at(x, lax.div(p, NZ), lax.rem(p, NZ), wt) for p in cols]
    side_dev = [at(x, y, z, lax.rem(wt + n, 4)) for n in range(1, 4)]
    peers = {
        "x+": at(lax.rem(x + 1, NX), y, z, wt),
        "x-": at(lax.rem(x + NX - 1, NX), y, z, wt),
        "z+": at(x, y, lax.rem(z + 1, NZ), wt),
        "z-": at(x, y, lax.rem(z + NZ - 1, NZ), wt),
        "y": at(x, 1 - y, z, wt),
    }
    barrier = pltpu.get_barrier_semaphore()
    partners = row_dev + col_dev + side_dev
    for peer in partners:
        pl.semaphore_signal(barrier, inc=1, device_id=peer, device_id_type=MESH)
    loads = [
        pltpu.make_async_copy(a, b, lsem.at[n])
        for n, (a, b) in enumerate(
            [(tok_hbm, tok), (q_hbm, q), (k_hbm, k), (gate_hbm, gate), (tgt_hbm, tgt)]
        )
    ]
    for c in (1, 2, 0, 3, 4):
        loads[c].start()

    squash = jax.nn.sigmoid(rv_ref[...])
    raw = 1.2 * squash - 0.1
    w_own[...] = (
        cs_ref[...] * (gb_ref[...].astype(F32) + jnp.clip(raw, 0.0, 1.0))
    ).astype(BF)
    factor[...] = cs_ref[...] * jnp.where(
        (raw > 0.0) & (raw < 1.0), 1.2 * squash * (1.0 - squash), 0.0
    )
    pl.semaphore_wait(barrier, len(partners))

    def rate_of(h, shape):
        return jnp.exp2(jnp.full(shape, -code_ref[h].astype(F32), F32))

    mult = [1.0 - 0.5 * bound_ref[c].astype(F32) for c in range(2)]

    def head_tables(h):
        lo = h * HEAD
        rate = rate_of(h, (1, HEAD))
        row = lax.broadcasted_iota(jnp.int32, (GROUP, HEAD), 0).astype(F32)
        qdec = jnp.exp(-(row * rate))
        kdec = jnp.exp(-((GROUP - row) * rate))
        i = lax.broadcasted_iota(jnp.int32, (GROUP, GROUP), 0)
        o = lax.broadcasted_iota(jnp.int32, (GROUP, GROUP), 1)
        gap = (i - o).astype(F32)
        causal = jnp.where(
            gap >= 0.0, jnp.exp(-(jnp.maximum(gap, 0.0) * rate_of(h, (1, GROUP)))), 0.0
        )
        rates[h * 8 : h * 8 + 8] = jnp.broadcast_to(jnp.exp(-GROUP * rate)[None], (8, 1, HEAD))
        for c in range(2):
            r = slice(c * GROUP, c * GROUP + GROUP)
            qh = q[r, lo : lo + HEAD]
            kh = k[r, lo : lo + HEAD]
            score = lax.dot_general(qh, kh, (((1,), (1,)), ((), ())), preferred_element_type=F32)
            wts[c, h] = (score * causal).astype(BF)
            qd[r, lo : lo + HEAD] = (qh.astype(F32) * qdec).astype(BF)
            kd[r, lo : lo + HEAD] = (kh.astype(F32) * kdec).astype(BF)

    def open_gates():
        go[...] = jax.nn.sigmoid(gate[...].astype(F32))

    fillers = [functools.partial(head_tables, h) for h in range(8)] + [open_gates]
    ready = [False]

    def filler():
        if not fillers:
            return
        if not ready[0]:
            for c in (1, 2, 3):
                loads[c].wait()
            ready[0] = True
        fillers.pop(0)()

    buf = (wa, wb)
    copies = {}
    tok_ready = False
    for n, op in enumerate(gplan):
        if op[0] == "send":
            _, sid, color, link, oz, ox, half = op
            w = buf[color]
            if link == "y":
                lo, hi = LANES[color]
                src = w_own.at[:, lo:hi]
                dst = w.at[y, z, x]
            else:
                zz = lax.rem(z + (oz + 2 * NZ), NZ)
                xx = lax.rem(x + (ox + 2 * NX), NX)
                dst = w.at[:, zz, xx] if half is None else w.at[half, zz, xx]
                src = dst
            copies[sid] = send(src, dst, gs.at[sid], gr.at[sid], peers[link])
            if len(copies) == 2:
                wa[y, z, x] = w_own[:, :SPLIT]
                wb[y, z, x] = w_own[:, SPLIT:]
                acc[...] = jnp.zeros_like(acc)
        elif op[0] == "recv":
            copies[op[1]].wait_recv()
        else:
            if not tok_ready:
                loads[0].wait()
                tok_ready = True
            _, color, oz = op
            zz = lax.rem(z + oz, NZ)
            lo, hi = LANES[color]
            w = buf[color]

            @pl.loop(0, 4)
            def _(i, zz=zz, lo=lo, hi=hi, w=w):
                r = pl.ds(pl.multiple_of(i * 128, 128), 128)
                t0 = tok[r, pl.ds(pl.multiple_of(zz * 256, 256), 256)]
                t1 = tok[r, pl.ds(pl.multiple_of(zz * 256 + 2048, 256), 256)]
                acc[r, lo:hi] += jnp.dot(
                    t0, w[0, zz].reshape(256, hi - lo), preferred_element_type=F32
                ) + jnp.dot(t1, w[1, zz].reshape(256, hi - lo), preferred_element_type=F32)
        if n >= 12 and n % 8 == 4:
            filler()
    while fillers:
        filler()

    def scan(f, reverse, meanwhile):
        one = [
            send(packed.at[f, p], xbuf.at[f, x], s1.at[f, n], r1.at[f, n], d)
            for n, (p, d) in enumerate(zip(rows, row_dev))
        ]
        xbuf[f, x] = packed[f, x]
        meanwhile()
        rate = rates[pl.ds(x * 16, 16)]
        rate = rate * rate
        rate1 = rates[x * 16 + j]
        rate1 = rate1 * rate1
        rate4 = (rate1 * rate1) * (rate1 * rate1)
        for c in one:
            c.wait_recv()
        order = list(reversed(range(NX))) if reverse else list(range(NX))
        total = jnp.zeros((16, 16, 128), F32)
        m_all = jnp.ones((16, 128), F32)
        mults = []
        for i in order:
            pref[i] = total
            mults.append(m_all)
            m = xbuf[f, i, 16].astype(F32)
            total = (rate * m[None]) * total + xbuf[f, i, pl.ds(0, 16)].astype(F32)
            m_all = m_all * m
        tbuf[f, :, 0] = total.astype(BF)
        tbuf[f, :, 1] = jnp.broadcast_to(m_all.astype(BF)[None], (16, 16, 128))
        two = [
            send(tbuf.at[f, p], ybuf.at[f, j], s2.at[f, n], r2.at[f, n], d)
            for n, (p, d) in enumerate(zip(cols, col_dev))
        ]
        ybuf[f, j] = tbuf[f, j]
        for c in two:
            c.wait_recv()
        state = jnp.zeros((16, 128), F32)
        span = NY * NZ
        for i in reversed(range(span)) if reverse else range(span):
            zbuf[f, i] = state.astype(BF)
            state = (rate4 * ybuf[f, i, 1].astype(F32)) * state + ybuf[f, i, 0].astype(F32)
        three = [
            send(zbuf.at[f, p], rbuf.at[f, j], s3.at[f, n], r3.at[f, n], d)
            for n, (p, d) in enumerate(zip(cols, col_dev))
        ]
        rbuf[f, j] = zbuf[f, j]
        for c in three:
            c.wait_recv()
        entering = rbuf[f].astype(F32)
        grow = jnp.ones((16, 1, 128), F32)
        for n, i in enumerate(order):
            obuf[f, i] = (pref[i] + (grow * mults[n][None]) * entering).astype(BF)
            grow = grow * rate
        four = [
            send(obuf.at[f, p], ebuf.at[f, x], s4.at[f, n], r4.at[f, n], d)
            for n, (p, d) in enumerate(zip(rows, row_dev))
        ]
        ebuf[f, x] = obuf[f, x]
        for c in four:
            c.wait_recv()
        return one + two + three + four

    def pack(f, h, part):
        packed[f, h // 2, (h % 2) * 8 : (h % 2) * 8 + 8] = part.astype(BF).reshape(8, 16, 128)

    def entered(f, h):
        return ebuf[f, h // 2, (h % 2) * 8 : (h % 2) * 8 + 8].reshape(HEAD, HEAD).astype(F32)

    def span_of(c, h):
        return slice(c * GROUP, c * GROUP + GROUP), slice(h * HEAD, h * HEAD + HEAD)

    for f in range(2):
        for n in range(NX):
            packed[f, n, 16] = jnp.full((16, 128), mult[0] * mult[1], F32).astype(BF)
    for h in range(8):
        fade = rates[h * 8]
        for c in range(2):
            r, l = span_of(c, h)
            v[r, l] = acc[r, l].astype(BF)
        u0 = tdot(kd[span_of(0, h)], v[span_of(0, h)])
        u1 = tdot(kd[span_of(1, h)], v[span_of(1, h)])
        hold[h] = u0
        pack(0, h, (fade * mult[1]) * u0 + u1)

    def intra():
        for h in range(8):
            for c in range(2):
                r, l = span_of(c, h)
                acc[r, l] = jnp.dot(wts[c, h], v[r, l], preferred_element_type=F32)

    scans = scan(0, False, intra)

    sums[12:16] = jnp.zeros((4, 128), F32)
    loads[4].wait()
    for c in range(2):
        square = jnp.zeros((GROUP, HEAD), F32)
        opened = jnp.zeros((GROUP, HEAD), F32)
        cross = jnp.zeros((GROUP, HEAD), F32)
        for h in range(8):
            r, l = span_of(c, h)
            fade = rates[h * 8]
            if c == 0:
                state = mult[0] * entered(0, h)
            else:
                state = mult[1] * hold[h] + (fade * (mult[0] * mult[1])) * entered(0, h)
            attn = acc[r, l] + jnp.dot(qd[r, l], state.astype(BF), preferred_element_type=F32)
            acc[r, l] = attn
            gated = attn * go[r, l]
            square = square + attn * attn
            opened = opened + gated * gated
            cross = cross + gated * tgt[r, l].astype(F32)
        for kind, part in enumerate((square, opened, cross)):
            for b in range(2):
                block = part[b * 128 : b * 128 + 128].T
                n = kind * 4 + c * 2 + b
                sums[n : n + 1] = jnp.sum(block, axis=0, keepdims=True)
    side = [
        send(sums, got.at[wt], ps.at[n], pr.at[n], d) for n, d in enumerate(side_dev)
    ]
    got[wt] = sums[...]
    for c in side:
        c.wait_recv()
    total = (got[0] + got[1]) + (got[2] + got[3])
    width = HEADS * HEAD
    inv_row = 1.0 / jnp.sqrt(total[0:4] / width + epsilon)
    inner_row = (scale * (total[4:8] * inv_row - total[8:12]) * inv_row) / width
    for n in range(4):
        r = slice(n * 128, n * 128 + 128)
        inv[r] = jnp.broadcast_to(inv_row[n : n + 1], (128, 128)).T
        inn[r] = jnp.broadcast_to(inner_row[n : n + 1], (128, 128)).T
    out_buf = q
    for h in range(8):
        fade = rates[h * 8]
        for c in range(2):
            r, l = span_of(c, h)
            normed = acc[r, l] * inv[r]
            gate_open = go[r, l]
            gated = normed * gate_open
            out_buf[r, l] = gated.astype(BF)
            grad_normed = ((gated - tgt[r, l].astype(F32)) * scale) * gate_open
            ga[r, l] = ((grad_normed - normed * inn[r]) * inv[r]).astype(BF)
        c0 = tdot(qd[span_of(0, h)], ga[span_of(0, h)])
        c1 = tdot(qd[span_of(1, h)], ga[span_of(1, h)])
        hold[h] = c1
        pack(1, h, mult[0] * c0 + (fade * (mult[0] * mult[1])) * c1)
    store = pltpu.make_async_copy(out_buf, gated_hbm, lsem.at[5])
    store.start()

    def back_intra():
        for h in range(8):
            for c in range(2):
                r, l = span_of(c, h)
                acc[r, l] = tdot(wts[c, h], ga[r, l])
        for c in copies.values():
            c.wait_send()

    scans += scan(1, True, back_intra)
    for h in range(8):
        fade = rates[h * 8]
        for c in range(2):
            r, l = span_of(c, h)
            state = entered(1, h)
            if c == 0:
                state = mult[1] * hold[h] + (fade * mult[1]) * state
            gv[r, l] = (
                acc[r, l] + jnp.dot(kd[r, l], state.astype(BF), preferred_element_type=F32)
            ).astype(BF)

    mine = (wa, wb)
    queue = (qa, qb)
    slots = {(0, 1): ra1, (1, 1): rb1, (0, 2): ra2, (1, 2): rb2}
    full = (fa, fb)
    ysend = (ya, yb)
    yrecv = (va, vb)
    moves = {}

    def slot(color, stage, flow, inst, n):
        r = slots[color, stage]
        f = 0 if flow < 0 else 1
        return r.at[f, inst, n] if stage == 1 else r.at[f, n]

    def own(color, stage, inst, there):
        if stage == 2:
            return queue[color].at[there]
        oz, ox = (there, inst) if color == 0 else (inst, there)
        return mine[color].at[:, lax.rem(z + oz, NZ), lax.rem(x + ox, NX)]

    for op in rplan:
        if op[0] == "chunk":
            zz = lax.rem(z + op[1], NZ)

            @pl.loop(0, 4)
            def _(i, zz=zz):
                yy = lax.div(i, 2)
                b = lax.rem(i, 2)
                piece = tok[:, pl.ds(pl.multiple_of(yy * 2048 + zz * 256 + b * 128, 128), 128)]
                r = tdot(piece, gv[...]).astype(BF)
                for u in range(2):
                    wa[yy, zz, b * 2 + u] = r[u * 64 : u * 64 + 64, :SPLIT]
                    wb[yy, zz, b * 2 + u] = r[u * 64 : u * 64 + 64, SPLIT:]
        elif op[0] == "s":
            _, color, stage, flow, inst, n = op
            axis, size = ring(color, stage)
            half = 0 if flow < 0 else 1
            p = own(color, stage, inst, (flow * n) % size)
            if n == size // 2:
                src = p.at[half]
                dst = slot(color, stage, flow, inst, n - 1).at[half]
            else:
                moves["s", color, stage, flow, inst, n + 1].wait_recv()
                src = slot(color, stage, flow, inst, n)
                dst = slot(color, stage, flow, inst, n - 1)
                if n == size // 2 - 1:
                    src[half] = (src[half].astype(F32) + p[half].astype(F32)).astype(BF)
                    src[1 - half] = p[1 - half]
                else:
                    src[...] = (src[...].astype(F32) + p[...].astype(F32)).astype(BF)
            sid = sids[op]
            link = axis + ("+" if flow > 0 else "-")
            moves[op] = send(src, dst, rs.at[sid], rr.at[sid], peers[link])
        elif op[0] == "q":
            _, color, stage, inst = op
            for flow in (-1, 1):
                moves["s", color, stage, flow, inst, 1].wait_recv()
            low = slot(color, stage, -1, inst, 0)
            high = slot(color, stage, 1, inst, 0)
            p = own(color, stage, inst, 0)
            total = low[...].astype(F32) + high[...].astype(F32) + p[...].astype(F32)
            if stage == 1:
                queue[color][inst] = total.astype(BF)
            else:
                full[color][...] = total
        elif op[0] == "y":
            color = op[1]
            ysend[color][...] = full[color][1 - y].astype(BF)
            sid = sids[op]
            moves[op] = send(ysend[color], yrecv[color], rs.at[sid], rr.at[sid], peers["y"])
        else:
            color = op[1]
            moves["y", color].wait_recv()
            lo, hi = LANES[color]
            out_ref[:, lo:hi] = factor[:, lo:hi] * (
                full[color][y] + yrecv[color][...].astype(F32)
            )
    store.wait()
    for c in scans + side + list(moves.values()):
        c.wait_send()


def on_device(
    tokens, round_var, grid_base, col_scale, queries, keys, gates, target, decay_code, boundary
):
    gplan, gn, _ = gather_plan()
    rplan, sids, _ = reduce_plan()
    rn = len(sids)
    scale = loss_weight / math.sqrt(tokens.shape[0] * lax.axis_size("ctx"))
    a, b = SPLIT, 1024 - SPLIT
    vm = pl.BlockSpec(memory_space=pltpu.VMEM)
    sm = pl.BlockSpec(memory_space=pltpu.SMEM)
    hbm = pl.BlockSpec(memory_space=pl.ANY)
    V = pltpu.VMEM
    D = pltpu.SemaphoreType.DMA
    scratch = [
        V((512, 4096), BF),
        V((512, 1024), BF), V((512, 1024), BF), V((512, 1024), BF), V((512, 1024), BF),
        V((64, 1024), BF), V((64, 1024), F32),
        V((NY, NZ, NX, 64, a), BF), V((NY, NZ, NX, 64, b), BF),
        V((512, 1024), F32), V((512, 1024), BF),
        V((2, 8, GROUP, GROUP), BF), V((512, 1024), BF), V((512, 1024), BF),
        V((512, 1024), F32), V((512, 1024), BF), V((512, 1024), BF),
        V((8, HEAD, HEAD), F32), V((64, 1, 128), F32),
        V((2, NX, 17, 16, 128), BF), V((2, NX, 17, 16, 128), BF),
        V((NX, 16, 16, 128), F32),
        V((2, 16, 2, 16, 128), BF), V((2, 16, 2, 16, 128), BF),
        V((2, 16, 16, 128), BF), V((2, 16, 16, 128), BF),
        V((2, NX, 16, 16, 128), BF), V((2, NX, 16, 16, 128), BF),
        V((16, 128), F32), V((4, 16, 128), F32),
        V((512, 128), F32), V((512, 128), F32),
        V((2, NX, NZ // 2, NY, 64, a), BF), V((2, NZ, NX // 2, NY, 64, b), BF),
        V((2, NX // 2, NY, 64, a), BF), V((2, NZ // 2, NY, 64, b), BF),
        V((NX, NY, 64, a), BF), V((NZ, NY, 64, b), BF),
        V((NY, 64, a), F32), V((NY, 64, b), F32),
        V((64, a), BF), V((64, b), BF), V((64, a), BF), V((64, b), BF),
        D((6,)), D((gn,)), D((gn,)),
        D((2, 3)), D((2, 3)), D((2, 15)), D((2, 15)), D((2, 15)), D((2, 15)), D((2, 3)), D((2, 3)),
        D((3,)), D((3,)), D((rn,)), D((rn,)),
    ]
    return pl.pallas_call(
        functools.partial(layer_kernel, gplan, rplan, sids, scale),
        out_shape=(
            jax.ShapeDtypeStruct((512, 1024), BF),
            jax.ShapeDtypeStruct((64, 1024), F32),
        ),
        in_specs=[sm, sm, vm, vm, vm, hbm, hbm, hbm, hbm, hbm],
        out_specs=(hbm, vm),
        scratch_shapes=scratch,
        compiler_params=pltpu.CompilerParams(
            collective_id=0, has_side_effects=True, vmem_limit_bytes=62 * 2**20
        ),
        name="layer_step",
    )(
        decay_code, boundary, round_var, grid_base, col_scale.reshape(1, -1), tokens, queries,
        keys, gates, target,
    )


def solution(mesh):
    placed = (
        P("ctx", None),
        P("ctx", "wt"),
        P("ctx", "wt"),
        P("wt"),
        P("ctx", "wt"),
        P("ctx", "wt"),
        P("ctx", "wt"),
        P("ctx", "wt"),
        P("wt"),
        P("ctx"),
    )
    return jax.shard_map(
        on_device,
        mesh=mesh,
        in_specs=placed,
        out_specs=(P("ctx", "wt"), P("ctx", "wt")),
        check_vma=False,
    )
```

time: 1670 us -> 178 us (0.11)
  waiting for transfers between devices: 1310 us -> 0 us
  blocking collectives: 177 us -> 0 us
  Pallas kernels: 0 us -> 173 us
  other arithmetic: 97.5 us -> 0 us
  matrix products: 30.2 us -> 0 us
  local copies, waits for them, and re-layouts: 32.3 us -> 3.93 us
    all_gather x3 -> x0, waiting for transfers between devices: 920 us -> none  [the longest x2 613 us: carried_in(): gathered = jax.tree.map(lambda a: lax.all_gather(a, axis), part)]
    reduce_scatter x1 -> x0, waiting for transfers between devices: 390 us -> none  [on_device(): lax.psum_scatter(full_term, 'ctx', scatter_dimension=0, tiled=True)]
    pallas_call x0 -> x1, Pallas kernels: none -> 173 us  [on_device(): pl.pallas_call(functools.partial(layer_kernel, gplan, rplan, sids, scale)...]
    unnamed x1 -> x0, blocking collectives: 160 us -> none
    add x64 -> x0, other arithmetic: 76.6 us -> none  [the longest x63 75.1 us: combine(): later[0][:, None, None] * earlier[1] + later[1]]
    dot_general x9 -> x0, matrix products: 30.2 us -> none  [the longest x1 10.4 us: on_device(): lax.dot_general(tokens, grad_values, (((0,), (0,)), ((), ())), preferred_...]
    unnamed x40 -> x2, local copies, waits for them, and re-layouts: 24.5 us -> 3.93 us
  transfers between devices with their start and end apart: 4 -> 0, of which waited for: 4 -> 0; matrix products, arithmetic and copies ran while one was open for 1% -> 0% of each run, Pallas kernels for 0% -> 0%
where the time goes in v2:
time: 178 us
  Pallas kernels  173 us (97%)
  local copies, waits for them, and re-layouts  3.93 us (2%)
    pallas_call x1, Pallas kernels, on_device(): pl.pallas_call(functools.partial(layer_kernel, gplan, rplan, sids, scale)...  173 us
    unnamed x2, local copies, waits for them, and re-layouts  3.93 us

profile of v2, /device:TPU:8, one launch (start us, length us, event | category | flops | bytes accessed | tf_op | source)
XLA Modules:
  0.0 178.0 jit_solution(12561718115999969150)
XLA Ops:
  0.6 173.4 %layer_step.1 = (bf16[512,1024]{1,0:T(8,128)(2,1)}, f32[64,1024]{1,0:T(8,128)}) custom-call(s32[8]{0:T(128)} %code_ref.1, s32[2]{0:T(128)} %bound_ref.1, f32[64,1024]{1,0:T(8,128)} %rv_ref.1, bf16[64,1024]{1,0:T(8,128)(2,1)} %gb_ref.1, f32[1,1024]{1,0:T(1,128)} %bitcast.1, bf16[512,4096]{1,0:T(8,128)(2,1)} %tok_hbm.1, bf16[512,1024]{1,0:T(8,128)(2,1)} %q_hbm.1, ...), custom_call_target="tpu_custom_call" | custom-call | tf_op jit(solution)/shard_map/layer_step/pallas_call | solution.py:633
  174.1 2.3 %copy.14 = bf16[512,1024]{1,0:T(8,128)(2,1)} copy(bf16[512,1024]{1,0:T(8,128)(2,1)} %get-tuple-element.4) | data formatting | bytes 2097152
  176.3 1.7 copy.15

commit v3 on v2

--- a/solution.py
+++ b/solution.py
@@ -122,43 +122,44 @@
     return plan, seq[0], max(links.free.values())
 
 
+COLOURS = (
+    (0, 256, False, "x"),
+    (256, 512, True, "z"),
+    (512, 896, True, "x"),
+    (896, 1024, True, "z"),
+)
 CHUNKS = (4, 3, 5, 2, 6, 1, 7, 0)
 CHUNK_US = 1.3
 
-
-def ring(color, stage):
-    axis = ("z", "x") if color == 0 else ("x", "z")
-    return axis[stage - 1], {"x": NX, "z": NZ}[axis[stage - 1]]
-
-
-def reduce_plan():
-    width = {0: SPLIT, 1: 1024 - SPLIT}
+def ring(first, stage):
+    axis = first if stage == 1 else ("x" if first == "z" else "z")
+    return axis, {"x": NX, "z": NZ}[axis]
+
+
+def reduce_plan(colours):
     links = Links()
     needs = {}
-    inst_of = {(0, 1): (2, 1, 3, 0), (1, 1): CHUNKS, (0, 2): (0,), (1, 2): (0,)}
-    for color in (1, 0):
+    for color, (lo, hi, paired, first) in enumerate(colours):
         for stage in (1, 2):
-            axis, n = ring(color, stage)
-            for inst in inst_of[color, stage]:
+            axis, n = ring(first, stage)
+            insts = (0,) if stage == 2 else (2, 1, 3, 0) if first == "z" else CHUNKS
+            for inst in insts:
                 for flow in (-1, 1):
                     for k in range(n // 2, 0, -1):
-                        task = ("s", color, stage, flow, inst, k)
                         there = (flow * k) % n
                         if stage == 1:
-                            dep = [("chunk", there if color == 0 else inst)]
+                            dep = [("chunk", color, there if first == "z" else inst)]
                         else:
                             dep = [("q", color, 1, there)]
                         if k < n // 2:
                             dep.append(("got", color, stage, flow, inst, k + 1))
-                        needs[task] = dep
+                        needs["s", color, stage, flow, inst, k] = dep
                 dep = [("got", color, stage, flow, inst, 1) for flow in (-1, 1)]
-                if stage == 1:
-                    dep.append(("chunk", 0 if color == 0 else inst))
-                else:
-                    dep.append(("q", color, 1, 0))
-                needs[("q", color, stage, inst)] = dep
-        needs[("y", color)] = [("q", color, 2, 0)]
-        needs[("out", color)] = [("goty", color)]
+                dep.append(("chunk", color, 0 if first == "z" else inst) if stage == 1 else ("q", color, 1, 0))
+                needs["q", color, stage, inst] = dep
+        if not paired:
+            needs["y", color] = [("q", color, 2, 0)]
+            needs["out", color] = [("goty", color)]
     done = set()
     plan = []
     heap = []
@@ -168,8 +169,13 @@
         seq[0] += 1
         heapq.heappush(heap, (t, seq[0], event))
 
-    for i, oz in enumerate(CHUNKS):
-        post(CHUNK_US * (i + 1), ("chunk", oz))
+    core = 0.0
+    for color, (lo, hi, paired, _) in enumerate(colours):
+        if paired:
+            core = max(core, links.send("y", 0.0, 512 * (hi - lo) * 2))
+        for oz in CHUNKS:
+            core += CHUNK_US * (hi - lo) / 1024
+            post(core, ("chunk", color, oz))
     sids = {}
     last = 0.0
     while heap:
@@ -182,22 +188,24 @@
         while moved:
             moved = False
             for task in list(needs):
-                if all(d in done for d in needs[task]):
-                    del needs[task]
-                    plan.append(task)
-                    moved = True
-                    if task[0] == "s":
-                        _, color, stage, flow, inst, k = task
-                        axis, n = ring(color, stage)
-                        halves = 1 if k == n // 2 else 2
-                        arrive = links.send((axis, flow), t, halves * 64 * width[color] * 2)
-                        post(arrive, ("got",) + task[1:])
-                        sids[task] = len(sids)
-                    elif task[0] == "y":
-                        post(links.send("y", t, 64 * width[task[1]] * 2), ("goty", task[1]))
-                        sids[task] = len(sids)
-                    elif task[0] == "q":
-                        done.add(task)
+                if not all(d in done for d in needs[task]):
+                    continue
+                del needs[task]
+                plan.append(task)
+                moved = True
+                width = colours[task[1]][1] - colours[task[1]][0]
+                rows = 32 if colours[task[1]][2] else 64
+                if task[0] == "s":
+                    _, color, stage, flow, inst, k = task
+                    axis, n = ring(colours[color][3], stage)
+                    halves = 1 if k == n // 2 else 2
+                    post(links.send((axis, flow), t, halves * rows * width * 2), ("got",) + task[1:])
+                    sids[task] = len(sids)
+                elif task[0] == "y":
+                    post(links.send("y", t, 64 * width * 2), ("goty", task[1]))
+                    sids[task] = len(sids)
+                elif task[0] == "q":
+                    done.add(task)
     return plan, sids, last
 
 
@@ -219,8 +227,9 @@
     gated_hbm, out_ref,
     tok, q, k, gate, tgt, w_own, factor, wa, wb, acc, v, wts, qd, kd, go, ga, gv, hold, rates,
     packed, xbuf, pref, tbuf, ybuf, zbuf, rbuf, obuf, ebuf, sums, got, inv, inn,
-    ra1, rb1, ra2, rb2, qa, qb, fa, fb, ya, yb, va, vb,
-    lsem, gs, gr, s1, r1, s2, r2, s3, r3, s4, r4, ps, pr, rs, rr,
+    tp, gp,
+    lsem, gs, gr, s1, r1, s2, r2, s3, r3, s4, r4, ps, pr, rs, rr, ts, tr, us, ur, hs, hr,
+    *lots,
 ):
     x, y, z, wt = place()
     j = y * NZ + z
@@ -346,7 +355,19 @@
     while fillers:
         filler()
 
-    def scan(f, reverse, meanwhile):
+    core = lax.rem(wt, 2)
+    twin = at(x, y, z, wt + 1 - 2 * core)
+    trade = []
+
+    def trade_tokens(first, last):
+        for n in range(first, last):
+            r = pl.ds(pl.multiple_of(core * 256 + n * 32, 32), 32)
+            src = tok.at[r, pl.ds(pl.multiple_of((1 - y) * 2048, 2048), 2048)]
+            trade.append(send(src, tp.at[r], ts.at[n], tr.at[n], peers["y"]))
+
+    trade_tokens(0, 2)
+
+    def scan(f, reverse, meanwhile, later):
         one = [
             send(packed.at[f, p], xbuf.at[f, x], s1.at[f, n], r1.at[f, n], d)
             for n, (p, d) in enumerate(zip(rows, row_dev))
@@ -391,6 +412,7 @@
         rbuf[f, j] = zbuf[f, j]
         for c in three:
             c.wait_recv()
+        later()
         entering = rbuf[f].astype(F32)
         grow = jnp.ones((16, 1, 128), F32)
         for n, i in enumerate(order):
@@ -433,7 +455,7 @@
                 r, l = span_of(c, h)
                 acc[r, l] = jnp.dot(wts[c, h], v[r, l], preferred_element_type=F32)
 
-    scans = scan(0, False, intra)
+    scans = scan(0, False, intra, lambda: trade_tokens(2, 8))
 
     sums[12:16] = jnp.zeros((4, 128), F32)
     loads[4].wait()
@@ -496,11 +518,16 @@
             for c in range(2):
                 r, l = span_of(c, h)
                 acc[r, l] = tdot(wts[c, h], ga[r, l])
-        for c in copies.values():
-            c.wait_send()
-
-    scans += scan(1, True, back_intra)
-    for h in range(8):
+        for n, c in enumerate(trade):
+            c.wait_recv()
+            r = pl.ds(pl.multiple_of(core * 256 + n * 32, 32), 32)
+            share.append(send(tp.at[r], tp.at[r], us.at[n], ur.at[n], twin))
+
+    share = []
+    scans += scan(1, True, back_intra, lambda: None)
+    grads = {}
+
+    def value_grads(h):
         fade = rates[h * 8]
         for c in range(2):
             r, l = span_of(c, h)
@@ -511,41 +538,63 @@
                 acc[r, l] + jnp.dot(kd[r, l], state.astype(BF), preferred_element_type=F32)
             ).astype(BF)
 
-    mine = (wa, wb)
-    queue = (qa, qb)
-    slots = {(0, 1): ra1, (1, 1): rb1, (0, 2): ra2, (1, 2): rb2}
-    full = (fa, fb)
-    ysend = (ya, yb)
-    yrecv = (va, vb)
+    for color, (lo, hi, paired, _) in sorted(enumerate(COLOURS), key=lambda e: not e[1][2]):
+        for h in range(lo // HEAD, hi // HEAD):
+            value_grads(h)
+        if paired:
+            grads[color] = send(
+                gv.at[:, lo:hi], gp.at[:, lo:hi], hs.at[color], hr.at[color], peers["y"]
+            )
+
+    bufs = [lots[n : n + 7] for n in range(0, len(lots), 7)]
     moves = {}
+    arrived = set()
 
     def slot(color, stage, flow, inst, n):
-        r = slots[color, stage]
+        r = bufs[color][stage]
         f = 0 if flow < 0 else 1
         return r.at[f, inst, n] if stage == 1 else r.at[f, n]
 
     def own(color, stage, inst, there):
         if stage == 2:
-            return queue[color].at[there]
-        oz, ox = (there, inst) if color == 0 else (inst, there)
-        return mine[color].at[:, lax.rem(z + oz, NZ), lax.rem(x + ox, NX)]
+            return bufs[color][3].at[there]
+        oz, ox = (there, inst) if COLOURS[color][3] == "z" else (inst, there)
+        return bufs[color][0].at[lax.rem(z + oz, NZ), lax.rem(x + ox, NX)]
 
     for op in rplan:
+        color = op[1]
+        lo, hi, paired, first = COLOURS[color]
         if op[0] == "chunk":
-            zz = lax.rem(z + op[1], NZ)
-
-            @pl.loop(0, 4)
-            def _(i, zz=zz):
-                yy = lax.div(i, 2)
-                b = lax.rem(i, 2)
-                piece = tok[:, pl.ds(pl.multiple_of(yy * 2048 + zz * 256 + b * 128, 128), 128)]
-                r = tdot(piece, gv[...]).astype(BF)
-                for u in range(2):
-                    wa[yy, zz, b * 2 + u] = r[u * 64 : u * 64 + 64, :SPLIT]
-                    wb[yy, zz, b * 2 + u] = r[u * 64 : u * 64 + 64, SPLIT:]
+            zz = lax.rem(z + op[2], NZ)
+            part = bufs[color][0]
+            if paired:
+                if not arrived:
+                    for c in share:
+                        c.wait_recv()
+                if color not in arrived:
+                    grads[color].wait_recv()
+                    arrived.add(color)
+
+                @pl.loop(0, 2)
+                def _(b, zz=zz, lo=lo, hi=hi, part=part):
+                    mine = tok[:, pl.ds(pl.multiple_of(y * 2048 + zz * 256 + b * 128, 128), 128)]
+                    other = tp[:, pl.ds(pl.multiple_of(zz * 256 + b * 128, 128), 128)]
+                    r = (tdot(mine, gv[:, lo:hi]) + tdot(other, gp[:, lo:hi])).astype(BF)
+                    for u in range(2):
+                        part[zz, b * 2 + u] = r[u * 64 : u * 64 + 64].reshape(2, 32, hi - lo)
+            else:
+
+                @pl.loop(0, 4)
+                def _(i, zz=zz, lo=lo, hi=hi, part=part):
+                    yy = lax.div(i, 2)
+                    b = lax.rem(i, 2)
+                    mine = tok[:, pl.ds(pl.multiple_of(yy * 2048 + zz * 256 + b * 128, 128), 128)]
+                    r = tdot(mine, gv[:, lo:hi]).astype(BF)
+                    for u in range(2):
+                        part[zz, b * 2 + u, yy] = r[u * 64 : u * 64 + 64]
         elif op[0] == "s":
             _, color, stage, flow, inst, n = op
-            axis, size = ring(color, stage)
+            axis, size = ring(first, stage)
             half = 0 if flow < 0 else 1
             p = own(color, stage, inst, (flow * n) % size)
             if n == size // 2:
@@ -572,23 +621,25 @@
             p = own(color, stage, inst, 0)
             total = low[...].astype(F32) + high[...].astype(F32) + p[...].astype(F32)
             if stage == 1:
-                queue[color][inst] = total.astype(BF)
+                bufs[color][3][inst] = total.astype(BF)
+            elif paired:
+                out_ref[:, lo:hi] = factor[:, lo:hi] * total.reshape(64, hi - lo)
             else:
-                full[color][...] = total
+                bufs[color][4][...] = total
         elif op[0] == "y":
-            color = op[1]
-            ysend[color][...] = full[color][1 - y].astype(BF)
+            ysend, yrecv = bufs[color][5:7]
+            ysend[...] = bufs[color][4][1 - y].astype(BF)
             sid = sids[op]
-            moves[op] = send(ysend[color], yrecv[color], rs.at[sid], rr.at[sid], peers["y"])
+            moves[op] = send(ysend, yrecv, rs.at[sid], rr.at[sid], peers["y"])
         else:
-            color = op[1]
             moves["y", color].wait_recv()
-            lo, hi = LANES[color]
             out_ref[:, lo:hi] = factor[:, lo:hi] * (
-                full[color][y] + yrecv[color][...].astype(F32)
+                bufs[color][4][y] + bufs[color][6][...].astype(F32)
             )
     store.wait()
-    for c in scans + side + list(moves.values()):
+    for c in list(copies.values()) + scans + side + trade + share:
+        c.wait_send()
+    for c in list(grads.values()) + list(moves.values()):
         c.wait_send()
 
 
@@ -596,7 +647,7 @@
     tokens, round_var, grid_base, col_scale, queries, keys, gates, target, decay_code, boundary
 ):
     gplan, gn, _ = gather_plan()
-    rplan, sids, _ = reduce_plan()
+    rplan, sids, _ = reduce_plan(COLOURS)
     rn = len(sids)
     scale = loss_weight / math.sqrt(tokens.shape[0] * lax.axis_size("ctx"))
     a, b = SPLIT, 1024 - SPLIT
@@ -621,15 +672,21 @@
         V((2, NX, 16, 16, 128), BF), V((2, NX, 16, 16, 128), BF),
         V((16, 128), F32), V((4, 16, 128), F32),
         V((512, 128), F32), V((512, 128), F32),
-        V((2, NX, NZ // 2, NY, 64, a), BF), V((2, NZ, NX // 2, NY, 64, b), BF),
-        V((2, NX // 2, NY, 64, a), BF), V((2, NZ // 2, NY, 64, b), BF),
-        V((NX, NY, 64, a), BF), V((NZ, NY, 64, b), BF),
-        V((NY, 64, a), F32), V((NY, 64, b), F32),
-        V((64, a), BF), V((64, b), BF), V((64, a), BF), V((64, b), BF),
+        V((512, 2048), BF), V((512, 1024), BF),
         D((6,)), D((gn,)), D((gn,)),
         D((2, 3)), D((2, 3)), D((2, 15)), D((2, 15)), D((2, 15)), D((2, 15)), D((2, 3)), D((2, 3)),
         D((3,)), D((3,)), D((rn,)), D((rn,)),
+        D((8,)), D((8,)), D((8,)), D((8,)), D((len(COLOURS),)), D((len(COLOURS),)),
     ]
+    for lo, hi, paired, first in COLOURS:
+        r, w = 32 if paired else 64, hi - lo
+        n1, n2 = (NX, NZ) if first == "z" else (NZ, NX)
+        f = 8 if paired else 64
+        scratch += [
+            V((NZ, NX, 2, r, w), BF), V((2, n1, n2 // 2, 2, r, w), BF),
+            V((2, n1 // 2, 2, r, w), BF), V((n1, 2, r, w), BF),
+            V((2, f, w), F32), V((f, w), BF), V((f, w), BF),
+        ]
     return pl.pallas_call(
         functools.partial(layer_kernel, gplan, rplan, sids, scale),
         out_shape=(

time: 178 us -> 183 us (1.028)
  Pallas kernels: 173 us -> 177 us
    pallas_call x1, Pallas kernels: 173 us -> 177 us  [on_device(): pl.pallas_call(functools.partial(layer_kernel, gplan, rplan, sids, scale)...]
where the time goes in v3:
time: 183 us; the launch traced here: 182 us
  Pallas kernels  177 us (97%)
  local copies, waits for them, and re-layouts  3.93 us (2%)
    pallas_call x1, Pallas kernels, on_device(): pl.pallas_call(functools.partial(layer_kernel, gplan, rplan, sids, scale)...  177 us
    unnamed x2, local copies, waits for them, and re-layouts  3.93 us

profile of v3, /device:TPU:8, one launch (start us, length us, event | category | flops | bytes accessed | tf_op | source)
XLA Modules:
  0.0 182.0 jit_solution(11537746834027674980)
XLA Ops:
  0.6 177.5 %layer_step.1 = (bf16[512,1024]{1,0:T(8,128)(2,1)}, f32[64,1024]{1,0:T(8,128)}) custom-call(s32[8]{0:T(128)} %code_ref.1, s32[2]{0:T(128)} %bound_ref.1, f32[64,1024]{1,0:T(8,128)} %rv_ref.1, bf16[64,1024]{1,0:T(8,128)(2,1)} %gb_ref.1, f32[1,1024]{1,0:T(1,128)} %bitcast.1, bf16[512,4096]{1,0:T(8,128)(2,1)} %tok_hbm.1, bf16[512,1024]{1,0:T(8,128)(2,1)} %q_hbm.1, ...), custom_call_target="tpu_custom_call" | custom-call | tf_op jit(solution)/shard_map/layer_step/pallas_call | solution.py:690
  178.1 2.3 %copy.14 = bf16[512,1024]{1,0:T(8,128)(2,1)} copy(bf16[512,1024]{1,0:T(8,128)(2,1)} %get-tuple-element.4) | data formatting | bytes 2097152
  180.4 1.7 copy.15

commit v4 on v3

--- a/solution.py
+++ b/solution.py
@@ -125,11 +125,14 @@
 COLOURS = (
     (0, 256, False, "x"),
     (256, 512, True, "z"),
-    (512, 896, True, "x"),
-    (896, 1024, True, "z"),
+    (512, 640, True, "z"),
+    (640, 1024, True, "x"),
 )
 CHUNKS = (4, 3, 5, 2, 6, 1, 7, 0)
 CHUNK_US = 1.3
+TASK_US = 0.12
+ADD_RATE = 1e6
+
 
 def ring(first, stage):
     axis = first if stage == 1 else ("x" if first == "z" else "z")
@@ -142,15 +145,14 @@
     for color, (lo, hi, paired, first) in enumerate(colours):
         for stage in (1, 2):
             axis, n = ring(first, stage)
-            insts = (0,) if stage == 2 else (2, 1, 3, 0) if first == "z" else CHUNKS
-            for inst in insts:
+            for inst in CHUNKS if stage == 1 and first == "x" else (0,):
                 for flow in (-1, 1):
                     for k in range(n // 2, 0, -1):
                         there = (flow * k) % n
                         if stage == 1:
                             dep = [("chunk", color, there if first == "z" else inst)]
                         else:
-                            dep = [("q", color, 1, there)]
+                            dep = [("q", color, 1, there if first == "x" else 0)]
                         if k < n // 2:
                             dep.append(("got", color, stage, flow, inst, k + 1))
                         needs["s", color, stage, flow, inst, k] = dep
@@ -163,27 +165,31 @@
     done = set()
     plan = []
     heap = []
-    seq = [0]
+    seq = 0
 
     def post(t, event):
-        seq[0] += 1
-        heapq.heappush(heap, (t, seq[0], event))
-
+        nonlocal seq
+        seq += 1
+        heapq.heappush(heap, (t, seq, event))
+
+    queue = []
+    for color, (lo, hi, paired, _) in enumerate(colours):
+        ready = links.send("y", 0.0, 512 * (hi - lo) * 2) if paired else 0.0
+        queue += [(ready, ("chunk", color, oz)) for oz in CHUNKS]
+    post(*queue.pop(0))
+    sids = {}
     core = 0.0
-    for color, (lo, hi, paired, _) in enumerate(colours):
-        if paired:
-            core = max(core, links.send("y", 0.0, 512 * (hi - lo) * 2))
-        for oz in CHUNKS:
-            core += CHUNK_US * (hi - lo) / 1024
-            post(core, ("chunk", color, oz))
-    sids = {}
-    last = 0.0
     while heap:
         t, _, event = heapq.heappop(heap)
-        last = t
+        core = max(core, t)
         done.add(event)
         if event[0] == "chunk":
             plan.append(event)
+            lo, hi = colours[event[1]][:2]
+            core += CHUNK_US * (hi - lo) / 1024
+            if queue:
+                ready, nxt = queue.pop(0)
+                post(max(core, ready), nxt)
         moved = True
         while moved:
             moved = False
@@ -193,20 +199,25 @@
                 del needs[task]
                 plan.append(task)
                 moved = True
-                width = colours[task[1]][1] - colours[task[1]][0]
-                rows = 32 if colours[task[1]][2] else 64
+                lo, hi, paired, first = colours[task[1]]
+                rows = 32 if paired else 64
+                core += TASK_US
                 if task[0] == "s":
                     _, color, stage, flow, inst, k = task
-                    axis, n = ring(colours[color][3], stage)
-                    halves = 1 if k == n // 2 else 2
-                    post(links.send((axis, flow), t, halves * rows * width * 2), ("got",) + task[1:])
+                    axis, n = ring(first, stage)
+                    nbytes = (1 if k == n // 2 else 2) * rows * (hi - lo) * 2
+                    if stage == 1 and first == "z":
+                        nbytes *= NX
+                    if k < n // 2:
+                        core += nbytes / ADD_RATE
+                    post(links.send((axis, flow), core, nbytes), ("got",) + task[1:])
                     sids[task] = len(sids)
                 elif task[0] == "y":
-                    post(links.send("y", t, 64 * width * 2), ("goty", task[1]))
+                    post(links.send("y", core, 64 * (hi - lo) * 2), ("goty", task[1]))
                     sids[task] = len(sids)
                 elif task[0] == "q":
                     done.add(task)
-    return plan, sids, last
+    return plan, sids, core
 
 
 def send(src, dst, ssem, rsem, dev):
@@ -227,7 +238,7 @@
     gated_hbm, out_ref,
     tok, q, k, gate, tgt, w_own, factor, wa, wb, acc, v, wts, qd, kd, go, ga, gv, hold, rates,
     packed, xbuf, pref, tbuf, ybuf, zbuf, rbuf, obuf, ebuf, sums, got, inv, inn,
-    tp, gp,
+    tok_t, tp, gp,
     lsem, gs, gr, s1, r1, s2, r2, s3, r3, s4, r4, ps, pr, rs, rr, ts, tr, us, ur, hs, hr,
     *lots,
 ):
@@ -298,21 +309,20 @@
     def open_gates():
         go[...] = jax.nn.sigmoid(gate[...].astype(F32))
 
+    def turn_tokens(n):
+        tok_t[n * 512 : n * 512 + 512] = tok[:, n * 512 : n * 512 + 512].T
+
     fillers = [functools.partial(head_tables, h) for h in range(8)] + [open_gates]
-    ready = [False]
-
+    fillers += [functools.partial(turn_tokens, n) for n in range(8)]
     def filler():
-        if not fillers:
-            return
-        if not ready[0]:
-            for c in (1, 2, 3):
+        if len(fillers) == 17:
+            for c in (0, 1, 2, 3):
                 loads[c].wait()
-            ready[0] = True
-        fillers.pop(0)()
+        if fillers:
+            fillers.pop(0)()
 
     buf = (wa, wb)
     copies = {}
-    tok_ready = False
     for n, op in enumerate(gplan):
         if op[0] == "send":
             _, sid, color, link, oz, ox, half = op
@@ -334,9 +344,6 @@
         elif op[0] == "recv":
             copies[op[1]].wait_recv()
         else:
-            if not tok_ready:
-                loads[0].wait()
-                tok_ready = True
             _, color, oz = op
             zz = lax.rem(z + oz, NZ)
             lo, hi = LANES[color]
@@ -350,7 +357,7 @@
                 acc[r, lo:hi] += jnp.dot(
                     t0, w[0, zz].reshape(256, hi - lo), preferred_element_type=F32
                 ) + jnp.dot(t1, w[1, zz].reshape(256, hi - lo), preferred_element_type=F32)
-        if n >= 12 and n % 8 == 4:
+        if n >= 12 and n % 8 == 4 or n == 14:
             filler()
     while fillers:
         filler()
@@ -361,8 +368,8 @@
 
     def trade_tokens(first, last):
         for n in range(first, last):
-            r = pl.ds(pl.multiple_of(core * 256 + n * 32, 32), 32)
-            src = tok.at[r, pl.ds(pl.multiple_of((1 - y) * 2048, 2048), 2048)]
+            r = pl.ds(pl.multiple_of(core * 1024 + n * 128, 128), 128)
+            src = tok_t.at[pl.ds(pl.multiple_of((1 - y) * 2048 + core * 1024 + n * 128, 128), 128)]
             trade.append(send(src, tp.at[r], ts.at[n], tr.at[n], peers["y"]))
 
     trade_tokens(0, 2)
@@ -520,7 +527,7 @@
                 acc[r, l] = tdot(wts[c, h], ga[r, l])
         for n, c in enumerate(trade):
             c.wait_recv()
-            r = pl.ds(pl.multiple_of(core * 256 + n * 32, 32), 32)
+            r = pl.ds(pl.multiple_of(core * 1024 + n * 128, 128), 128)
             share.append(send(tp.at[r], tp.at[r], us.at[n], ur.at[n], twin))
 
     share = []
@@ -556,10 +563,13 @@
         return r.at[f, inst, n] if stage == 1 else r.at[f, n]
 
     def own(color, stage, inst, there):
+        if COLOURS[color][3] == "z":
+            if stage == 2:
+                return bufs[color][3].at[lax.rem(x + there, NX)]
+            return bufs[color][0].at[lax.rem(z + there, NZ)]
         if stage == 2:
             return bufs[color][3].at[there]
-        oz, ox = (there, inst) if COLOURS[color][3] == "z" else (inst, there)
-        return bufs[color][0].at[lax.rem(z + oz, NZ), lax.rem(x + ox, NX)]
+        return bufs[color][0].at[lax.rem(z + inst, NZ), lax.rem(x + there, NX)]
 
     for op in rplan:
         color = op[1]
@@ -575,27 +585,24 @@
                     grads[color].wait_recv()
                     arrived.add(color)
 
-                @pl.loop(0, 2)
-                def _(b, zz=zz, lo=lo, hi=hi, part=part):
-                    mine = tok[:, pl.ds(pl.multiple_of(y * 2048 + zz * 256 + b * 128, 128), 128)]
-                    other = tp[:, pl.ds(pl.multiple_of(zz * 256 + b * 128, 128), 128)]
-                    r = (tdot(mine, gv[:, lo:hi]) + tdot(other, gp[:, lo:hi])).astype(BF)
-                    for u in range(2):
-                        part[zz, b * 2 + u] = r[u * 64 : u * 64 + 64].reshape(2, 32, hi - lo)
+                mine = tok_t[pl.ds(pl.multiple_of(y * 2048 + zz * 256, 256), 256)]
+                other = tp[pl.ds(pl.multiple_of(zz * 256, 256), 256)]
+                r = jnp.dot(mine, gv[:, lo:hi], preferred_element_type=F32)
+                r = r + jnp.dot(other, gp[:, lo:hi], preferred_element_type=F32)
+                part[zz] = r.astype(BF).reshape(NX, 2, 32, hi - lo)
             else:
-
-                @pl.loop(0, 4)
-                def _(i, zz=zz, lo=lo, hi=hi, part=part):
-                    yy = lax.div(i, 2)
-                    b = lax.rem(i, 2)
-                    mine = tok[:, pl.ds(pl.multiple_of(yy * 2048 + zz * 256 + b * 128, 128), 128)]
-                    r = tdot(mine, gv[:, lo:hi]).astype(BF)
-                    for u in range(2):
-                        part[zz, b * 2 + u, yy] = r[u * 64 : u * 64 + 64]
+                for yy in range(2):
+                    mine = tok_t[pl.ds(pl.multiple_of(yy * 2048 + zz * 256, 256), 256)]
+                    r = jnp.dot(mine, gv[:, lo:hi], preferred_element_type=F32).astype(BF)
+                    for u in range(NX):
+                        part[zz, u, yy] = r[u * 64 : u * 64 + 64]
         elif op[0] == "s":
             _, color, stage, flow, inst, n = op
             axis, size = ring(first, stage)
             half = 0 if flow < 0 else 1
+            rest = 1 - half
+            if stage == 1 and first == "z":
+                half, rest = (slice(None), half), (slice(None), rest)
             p = own(color, stage, inst, (flow * n) % size)
             if n == size // 2:
                 src = p.at[half]
@@ -606,7 +613,7 @@
                 dst = slot(color, stage, flow, inst, n - 1)
                 if n == size // 2 - 1:
                     src[half] = (src[half].astype(F32) + p[half].astype(F32)).astype(BF)
-                    src[1 - half] = p[1 - half]
+                    src[rest] = p[rest]
                 else:
                     src[...] = (src[...].astype(F32) + p[...].astype(F32)).astype(BF)
             sid = sids[op]
@@ -620,7 +627,9 @@
             high = slot(color, stage, 1, inst, 0)
             p = own(color, stage, inst, 0)
             total = low[...].astype(F32) + high[...].astype(F32) + p[...].astype(F32)
-            if stage == 1:
+            if stage == 1 and first == "z":
+                bufs[color][3][...] = total.astype(BF)
+            elif stage == 1:
                 bufs[color][3][inst] = total.astype(BF)
             elif paired:
                 out_ref[:, lo:hi] = factor[:, lo:hi] * total.reshape(64, hi - lo)
@@ -672,7 +681,7 @@
         V((2, NX, 16, 16, 128), BF), V((2, NX, 16, 16, 128), BF),
         V((16, 128), F32), V((4, 16, 128), F32),
         V((512, 128), F32), V((512, 128), F32),
-        V((512, 2048), BF), V((512, 1024), BF),
+        V((4096, 512), BF), V((2048, 512), BF), V((512, 1024), BF),
         D((6,)), D((gn,)), D((gn,)),
         D((2, 3)), D((2, 3)), D((2, 15)), D((2, 15)), D((2, 15)), D((2, 15)), D((2, 3)), D((2, 3)),
         D((3,)), D((3,)), D((rn,)), D((rn,)),
@@ -682,8 +691,9 @@
         r, w = 32 if paired else 64, hi - lo
         n1, n2 = (NX, NZ) if first == "z" else (NZ, NX)
         f = 8 if paired else 64
+        lot = (2, 1, n2 // 2, NX, 2, r, w) if first == "z" else (2, n1, n2 // 2, 2, r, w)
         scratch += [
-            V((NZ, NX, 2, r, w), BF), V((2, n1, n2 // 2, 2, r, w), BF),
+            V((NZ, NX, 2, r, w), BF), V(lot, BF),
             V((2, n1 // 2, 2, r, w), BF), V((n1, 2, r, w), BF),
             V((2, f, w), F32), V((f, w), BF), V((f, w), BF),
         ]

time: 183 us -> 173 us (0.945)
  Pallas kernels: 177 us -> 168 us
    pallas_call x1, Pallas kernels: 177 us -> 168 us  [on_device(): pl.pallas_call(functools.partial(layer_kernel, gplan, rplan, sids, scale)...]
where the time goes in v4:
time: 173 us
  Pallas kernels  168 us (97%)
  local copies, waits for them, and re-layouts  3.93 us (2%)
    pallas_call x1, Pallas kernels, on_device(): pl.pallas_call(functools.partial(layer_kernel, gplan, rplan, sids, scale)...  168 us
    unnamed x2, local copies, waits for them, and re-layouts  3.93 us

profile of v4, /device:TPU:8, one launch (start us, length us, event | category | flops | bytes accessed | tf_op | source)
XLA Modules:
  0.0 172.8 jit_solution(17762579240075911907)
XLA Ops:
  0.6 168.2 %layer_step.1 = (bf16[512,1024]{1,0:T(8,128)(2,1)}, f32[64,1024]{1,0:T(8,128)}) custom-call(s32[8]{0:T(128)} %code_ref.1, s32[2]{0:T(128)} %bound_ref.1, f32[64,1024]{1,0:T(8,128)} %rv_ref.1, bf16[64,1024]{1,0:T(8,128)(2,1)} %gb_ref.1, f32[1,1024]{1,0:T(1,128)} %bitcast.1, bf16[512,4096]{1,0:T(8,128)(2,1)} %tok_hbm.1, bf16[512,1024]{1,0:T(8,128)(2,1)} %q_hbm.1, ...), custom_call_target="tpu_custom_call" | custom-call | tf_op jit(solution)/shard_map/layer_step/pallas_call | solution.py:700
  168.9 2.3 %copy.14 = bf16[512,1024]{1,0:T(8,128)(2,1)} copy(bf16[512,1024]{1,0:T(8,128)(2,1)} %get-tuple-element.4) | data formatting | bytes 2097152
  171.1 1.7 copy.15
